TPU v7x, 128 devices: a whole 4x4x4 slice. The times are simulated.
128 devices in a mesh: inst: 32 (over x, y, core), arch: 4 (over z).
Axes of the slice: x: 4, y: 4, z: 4, core: 2. Of those that a mesh axis runs over, the one named last changes fastest.
Arguments:
- instance_arch: int32 [8192], P(('inst', 'arch')), may hold values from 0 to 39
- instance_param: int32 [8192], P(('inst', 'arch')), may hold values from 0 to 1023
- instance_ports: int32 [8192, 4], P(('inst', 'arch')), may hold values from 0 to 16383, as said below
- port_row: int32 [16384], replicated, may hold values from 0 to 16383, as said below
- param_table: float32 [1024, 64], replicated, may hold values from 0.5 to 2
- bubble_inverse: float32 [40, 64, 64], P('arch'), as said below
- coupling: float32 [40, 64, 128], P('arch'), may hold values from -0.75 to 0.75
- port_stiffness: float32 [40, 128, 128], P('arch'), as said below
- coupling_offset: float32 [8192, 64, 128], P(('inst', 'arch')), may hold values from -0.375 to 0.375
Outputs:
- assembled: float32 [16384, 7168], P(('inst', 'arch'))
Inputs may be any that keep to these rules, and one draw needn't show every extreme that they name: `instance_ports`: every port is named exactly twice: once at slot 0 and once at slot 1 of two different instances, or once at slot 2 and once at slot 3 of two different instances; an instance's four ports are distinct. `port_row`: A permutation of the ports. Among the 256 port slots of one device's instances, at most 3 name ports whose row lies in one device's (128) rows, and this many is reached. `bubble_inverse`: each matrix is symmetric. `port_stiffness`: each matrix is symmetric.
All inputs are finite; a program needn't handle non-finite values.
Results may differ from a plain program's by a relative error of at most 0.00013.
Values sent between devices are 32-bit elements; how exact they have to be, the bound alone decides.
A program may use at most 128 MiB of HBM per device.

v0:
```python
import jax
import jax.numpy as jnp
import numpy as np
from jax import lax
from jax.sharding import PartitionSpec as P


def orders(width):
    result = []
    for which in range(4):
        parts = [np.arange(which * width, (which + 1) * width)]
        for other in range(4):
            if other != which:
                parts.append(np.arange(other * width, (other + 1) * width))
        result.append(np.concatenate(parts))
    return result


def condense(inverses, couplings, stiffness, table, arch_ids, param_ids, offsets):
    scales = jnp.take(table, param_ids, axis=0)
    weighted = scales[:, :, None] * (jnp.take(couplings, arch_ids, axis=0) + offsets)
    applied = jnp.einsum(
        "bmn,bnq->bmq",
        jnp.take(inverses, arch_ids, axis=0),
        weighted,
        precision=lax.Precision.HIGHEST,
    )
    return jnp.take(stiffness, arch_ids, axis=0) - jnp.einsum(
        "bmp,bmq->bpq", weighted, applied, precision=lax.Precision.HIGHEST
    )


def body(
    instance_arch,
    instance_param,
    instance_ports,
    port_row,
    param_table,
    bubble_inverse,
    coupling,
    port_stiffness,
    coupling_offset,
):
    instances = instance_arch.shape[0]
    width = port_stiffness.shape[1] // 4
    flat_width = 4 * width * width
    inverses, couplings, stiffness = (
        lax.all_gather(bubble_inverse, "arch", axis=0, tiled=True),
        lax.all_gather(coupling, "arch", axis=0, tiled=True),
        lax.all_gather(port_stiffness, "arch", axis=0, tiled=True),
    )
    schur = condense(
        inverses, couplings, stiffness, param_table, instance_arch, instance_param, coupling_offset
    )
    columns = orders(width)
    strips = jnp.concatenate(
        [
            schur[:, which * width : (which + 1) * width, :][:, :, columns[which]]
            for which in range(4)
        ],
        axis=0,
    )
    strips = strips.reshape(4 * instances, flat_width)
    row_ids = jnp.take(port_row, instance_ports, axis=0).T.reshape(4 * instances)
    slot_ids = jnp.repeat(jnp.arange(4, dtype=jnp.int32), instances)
    row_codes = row_ids * 4 + slot_ids
    inst_count = lax.axis_size("inst")
    arch_count = lax.axis_size("arch")
    owners = inst_count * arch_count
    port_count = 2 * instances
    capacity = 4 * instances // owners * 3 // 2
    owner_ids = row_ids // port_count
    owner_hits = (owner_ids[:, None] == jnp.arange(owners, dtype=jnp.int32)[None, :]).astype(
        jnp.int32
    )
    ordinal = jnp.sum((jnp.cumsum(owner_hits, axis=0) - 1) * owner_hits, axis=1)
    buffer_slot = owner_ids * capacity + ordinal
    chosen = buffer_slot[None, :] == jnp.arange(owners * capacity, dtype=jnp.int32)[:, None]
    outgoing = jnp.dot(
        chosen.astype(jnp.float32),
        strips,
        precision=lax.Precision.HIGHEST,
        preferred_element_type=jnp.float32,
    )
    filled = jnp.any(chosen, axis=1)
    out_codes = jnp.where(filled, jnp.sum(jnp.where(chosen, row_codes[None, :], 0), axis=1), -1)
    incoming, in_codes = (
        lax.all_to_all(
            outgoing.reshape(owners, capacity, flat_width),
            ("inst", "arch"),
            split_axis=0,
            concat_axis=0,
            tiled=True,
        ),
        lax.all_to_all(
            out_codes.reshape(owners, capacity),
            ("inst", "arch"),
            split_axis=0,
            concat_axis=0,
            tiled=True,
        ),
    )
    incoming = incoming.reshape(owners * capacity, flat_width)
    in_codes = in_codes.reshape(owners * capacity)
    my_index = lax.axis_index("inst") * arch_count + lax.axis_index("arch")
    live_slot = in_codes >= 0
    local_row = jnp.where(live_slot, in_codes // 4 - my_index * port_count, port_count)
    parity = in_codes % 4 % 2
    even_index = jnp.where(live_slot & (parity == 0), local_row, port_count)
    odd_index = jnp.where(live_slot & (parity == 1), local_row, port_count)
    targets = jnp.arange(port_count, dtype=jnp.int32)[:, None]
    placing = jnp.concatenate(
        [
            local_row[None, :] == targets,
            even_index[None, :] == targets,
            odd_index[None, :] == targets,
        ],
        axis=0,
    )
    placed = jnp.dot(
        placing.astype(jnp.float32),
        incoming,
        precision=lax.Precision.HIGHEST,
        preferred_element_type=jnp.float32,
    )
    placed = placed.reshape(3, port_count, width, 4 * width)
    joined = jnp.concatenate(
        [placed[0, :, :, :width], placed[1, :, :, width:], placed[2, :, :, width:]], axis=2
    )
    return joined.reshape(port_count, 7 * width * width)


def solution(mesh):
    return jax.shard_map(
        body,
        mesh=mesh,
        in_specs=(
            P(("inst", "arch")),
            P(("inst", "arch")),
            P(("inst", "arch"), None),
            P(),
            P(),
            P("arch", None, None),
            P("arch", None, None),
            P("arch", None, None),
            P(("inst", "arch"), None, None),
        ),
        out_specs=P(("inst", "arch"), None),
        check_vma=False,
    )
```

profile of v0, /device:TPU:6, one launch (start us, length us, event | category | flops | bytes accessed | tf_op | source)
XLA Modules:
  0.0 307.8 jit_solution(5884704730045930546)
XLA Ops:
  6.5 0.0 copy-start
  6.5 0.7 all-gather.5.cloned.1.call-update
  7.3 0.0 all-gather.3.cloned.1.call-start
  7.3 0.7 all-gather.3.cloned.1.call-update
  8.0 0.7 compare_select_fusion
  8.7 0.1 copy.92
  8.8 0.1 reshape.302
  8.9 0.0 copy-start.5
  8.9 0.0 copy-start.4
  8.9 0.0 copy-start.10
  9.0 1.7 gather_fusion
  10.7 0.0 copy-start.9
  10.7 0.0 copy-start.3
  10.7 0.1 reshape.301
  10.8 0.1 copy.93
  10.9 0.1 reshape.293
  11.0 0.1 copy.94
  11.1 0.2 fusion.9
  11.3 0.1 reshape.292
  11.4 0.1 reshape.295
  11.6 0.1 add_add_fusion
  11.7 0.2 fusion.10
  11.8 0.2 fusion.4
  12.0 0.1 select_reduce_fusion
  12.2 0.8 select_n.162
  13.0 10.5 %all-to-all-start = ((s32[128,1,3]{2,1,0:T(1,128)}), s32[128,1,3]{2,1,0:T(1,128)S(1)}, u32[]{:S(2)}, u32[]{:S(2)}) async-start(s32[128,1,3]{2,1,0:T(1,128)} %bitcast.4), calls=%async_computation | async-start | bytes 131072 | tf_op jit(solution)/shard_map/all_to_all | solution.py:95
  23.5 0.2 copy.97
  23.7 0.6 gather_fusion.2
  24.4 22.8 %all_gather.11 = f32[40,64,64]{2,1,0:T(8,128)S(1)} all-gather(f32[10,64,64]{2,1,0:T(8,128)S(1)} %copy-done.3), channel_id=1, replica_groups=mesh['inst'=32,'arch'=4] {'arch'}, dimensions={0}, use_global_device_ids=true | all-gather | bytes 819200 | tf_op jit(solution)/shard_map/all_gather | solution.py:48
  47.2 2.0 gather_fusion.4
  49.3 0.1 broadcast_select_fusion
  49.4 0.0 all-gather.5.cloned.1.call-done
  49.4 2.0 gather_fusion.3
  51.4 6.2 %fusion = f32[64,64,128]{2,1,0:T(8,128)} fusion(f32[64,64,64]{2,1,0:T(8,128)} %gather_fusion.4, pred[64]{0:T(512)(128)(4,1)S(1)} %compare_and_fusion.1, f32[64,64,128]{2,1,0:T(8,128)} %param.25, f32[64,64,128]{2,1,0:T(8,128)S(1)} %gather_fusion.3, f32[64,64]{1,0:T(8,128)S(1)} %broadcast_select_fusion), kind=kOutput, calls=%fused_computation.12 | convolution fusion | flops 404488192 | bytes 7356480 | tf_op jit(solution)/shard_map/bmn,bnq->bmq/dot_general | solution.py:22
  57.6 22.4 %all-gather.3.cloned.1.call-done = f32[40,128,128]{2,1,0:T(8,128)} async-done(((f32[10,128,128]{2,1,0:T(8,128)}), f32[40,128,128]{2,1,0:T(8,128)}) %all-gather.3.cloned.1.call-update) | async-done | bytes 2621456 | tf_op jit(solution)/shard_map/all_gather | solution.py:50
  79.9 4.6 %gather_fusion.1 = f32[64,128,128]{2,1,0:T(8,128)} fusion(f32[40,128,128]{2,1,0:T(8,128)} %all-gather.3.cloned.1.call-done, s32[1024]{0:T(1024)S(1)} %pad_clamp_fusion.5), kind=kCustom, calls=%fused_computation.1 | custom fusion | bytes 8388864 | tf_op jit(solution)/shard_map/jit(_take)/gather | solution.py:28
  84.6 11.6 %select_subtract_fusion = f32[64,128,128]{2,1,0:T(8,128)S(1)} fusion(f32[64,128,128]{2,1,0:T(8,128)} %gather_fusion.1, f32[64,64,128]{2,1,0:T(8,128)} %fusion, pred[64]{0:T(512)(128)(4,1)S(1)} %compare_and_fusion.1, f32[64,64,128]{2,1,0:T(8,128)} %param.25, f32[64,64,128]{2,1,0:T(8,128)S(1)} %gather_fusion.3, f32[64,64]{1,0:T(8,128)S(1)} %broadcast_select_fusion), kind=kOutput, calls=%fused_computation.10 | convolution fusion | flops 808976384 | bytes 14696512 | tf_op jit(solution)/shard_map/bmp,bmq->bpq/dot_general | solution.py:28
  96.1 1.4 fusion.20
  97.6 3.1 %copy.98 = f32[64,32,128]{0,1,2:T(8,128)} copy(f32[64,32,128]{2,1,0:T(8,128)S(1)} %get-tuple-element.9) | data formatting | bytes 2097152 | tf_op jit(solution)/shard_map/slice | solution.py:58
  100.7 2.9 copy.101
  103.6 3.0 copy.100
  106.7 2.9 copy.99
  109.6 3.6 %gather_fusion.5 = f32[128,64,32]{1,2,0:T(8,128)} fusion(f32[64,32,128]{0,1,2:T(8,128)} %copy.98, s32[1024]{0:T(1024)S(1)} %pad_clamp_fusion.3), kind=kCustom, calls=%fused_computation.5 | custom fusion | bytes 2097664 | tf_op jit(solution)/shard_map/gather | solution.py:58
  113.2 3.6 %gather_fusion.8 = f32[128,64,32]{1,2,0:T(8,128)} fusion(f32[64,32,128]{0,1,2:T(8,128)} %copy.101, s32[1024]{0:T(1024)S(1)} %pad_clamp_fusion), kind=kCustom, calls=%fused_computation.8 | custom fusion | bytes 2097664 | tf_op jit(solution)/shard_map/gather | solution.py:58
  116.8 2.1 gather_fusion.7
  118.9 3.7 %gather_fusion.6 = f32[128,64,32]{1,2,0:T(8,128)} fusion(f32[64,32,128]{0,1,2:T(8,128)} %copy.99, s32[1024]{0:T(1024)S(1)} %pad_clamp_fusion.2), kind=kCustom, calls=%fused_computation.6 | custom fusion | bytes 2097664 | tf_op jit(solution)/shard_map/gather | solution.py:58
  122.6 6.6 %pad_maximum_fusion = f32[256,32,128]{0,1,2:T(8,128)} fusion(f32[64,32,128]{0,1,2:T(8,128)} %bitcast.39, f32[64,32,128]{0,1,2:T(8,128)} %bitcast.40, f32[64,32,128]{0,1,2:T(8,128)} %bitcast.41, f32[64,32,128]{0,1,2:T(8,128)S(1)} %bitcast.38), kind=kLoop, calls=%fused_computation.9 | loop fusion | flops 3145728 | bytes 8388608 | tf_op jit(solution)/shard_map/concatenate | solution.py:56
  129.2 5.9 %copy.102 = f32[256,32,128]{2,1,0:T(8,128)} copy(f32[256,32,128]{0,1,2:T(8,128)} %pad_maximum_fusion) | data formatting | bytes 8388608 | tf_op jit(solution)/shard_map/concatenate | solution.py:56
  135.1 5.0 %reshape.378 = f32[256,4096,1]{1,0,2:T(8,128)} reshape(f32[256,32,128]{2,1,0:T(8,128)} %copy.102) | data formatting | bytes 8388608 | tf_op jit(solution)/shard_map/reshape | solution.py:63
  140.1 4.8 %fusion.5 = f32[128,3,4096]{2,0,1:T(8,128)S(1)} fusion(f32[256,4096,1]{1,0,2:T(8,128)} %reshape.378, s32[128,3]{0,1:T(4,128)S(1)} %multiply_add_fusion, s32[256]{0:T(256)S(1)} %multiply_add_fusion.2), kind=kOutput, calls=%fused_computation.24 | convolution fusion | flops 4831936512 | bytes 10488320 | tf_op jit(solution)/shard_map/dot_general | solution.py:79
  144.9 7.5 %copy.103 = f32[128,3,4096]{2,1,0:T(4,128)} copy(f32[128,3,4096]{2,0,1:T(8,128)S(1)} %fusion.5) | data formatting | bytes 12582912 | tf_op jit(solution)/shard_map/dot_general | solution.py:79
  152.5 0.0 all-to-all-done
  152.5 8.6 %all-to-all-start.1 = ((f32[128,3,4096]{2,1,0:T(4,128)}), f32[128,3,4096]{2,1,0:T(4,128)}, u32[]{:S(2)}, u32[]{:S(2)}) async-start(f32[128,3,4096]{2,1,0:T(4,128)} %copy.103), calls=%async_computation.1 | async-start | bytes 16777216 | tf_op jit(solution)/shard_map/all_to_all | solution.py:88
  161.1 0.5 broadcast.419
  161.6 0.8 reduce.3
  162.4 0.2 reshape.296
  162.7 0.1 iota_compare_fusion.2
  162.8 106.3 %all-to-all-done.1 = f32[128,3,4096]{2,1,0:T(4,128)} async-done(((f32[128,3,4096]{2,1,0:T(4,128)}), f32[128,3,4096]{2,1,0:T(4,128)}, u32[]{:S(2)}, u32[]{:S(2)}) %all-to-all-start.1) | async-done | bytes 6291488 | tf_op jit(solution)/shard_map/all_to_all | solution.py:88
  269.1 9.5 %reshape.298 = f32[384,4096]{1,0:T(8,128)} reshape(f32[128,3,4096]{2,1,0:T(4,128)} %all-to-all-done.1) | data formatting | bytes 12582912 | tf_op jit(solution)/shard_map/reshape | solution.py:103
  278.6 6.6 %copy.104 = f32[4096,384]{1,0:T(8,128)} copy(f32[4096,384]{0,1:T(8,128)} %bitcast.36) | data formatting | bytes 12582912 | tf_op jit(solution)/shard_map/dot_general | solution.py:120
  285.2 8.1 %fusion.21 = f32[3,128,32,128]{1,3,2,0:T(8,128)S(1)} fusion(pred[3,128,384,1]{2,1,3,0:T(32,128)(4,1)S(1)} %bitcast.42, f32[32,128,384,1]{2,1,0,3:T(8,128)} %bitcast.35), kind=kOutput, calls=%fused_computation.86 | convolution fusion | flops 7247757312 | bytes 12730368 | tf_op jit(solution)/shard_map/dot_general | solution.py:120
  293.4 0.3 slice_bitcast_fusion.1
  293.7 2.0 pad_maximum_fusion.1
  295.7 5.3 %copy.105 = f32[128,7168]{1,0:T(8,128)} copy(f32[128,7168]{0,1:T(8,128)} %bitcast.37) | data formatting | bytes 7340032 | tf_op jit(solution)/shard_map/reshape | solution.py:130
  (45 shorter events, 0.3 us)
Async XLA Ops:
  6.5 2.4 copy-start
  6.5 42.8 %all-gather.5.cloned.1.call-start = ((), (), s32[]{:S(2)}) async-start(), calls=%async_computation.3 | async-start | bytes 1638400 | tf_op jit(solution)/shard_map/all_gather | solution.py:49
  7.3 72.7 %all-gather.3.cloned.1.call-start = ((), (), s32[]{:S(2)}) async-start(), calls=%async_computation.2 | async-start | bytes 3276800 | tf_op jit(solution)/shard_map/all_gather | solution.py:50
  8.9 2.0 copy-start.5
  8.9 14.6 %copy-start.4 = (f32[1024,64]{0,1:T(8,128)S(1)}, f32[1024,64]{0,1:T(8,128)}, u32[]{:S(2)}) copy-start(f32[1024,64]{0,1:T(8,128)} %param.21) | copy-start | bytes 786436
  8.9 14.8 %copy-start.10 = (s32[64]{0:T(128)S(1)}, s32[64]{0:T(128)}, u32[]{:S(2)}) copy-start(s32[64]{0:T(128)} %param.18) | copy-start | bytes 772
  10.7 13.6 %copy-start.9 = (s32[64]{0:T(128)S(1)}, s32[64]{0:T(128)}, u32[]{:S(2)}) copy-start(s32[64]{0:T(128)} %param.17) | copy-start | bytes 772
  10.7 13.7 %copy-start.3 = (f32[10,64,64]{2,1,0:T(8,128)S(1)}, f32[10,64,64]{2,1,0:T(8,128)}, u32[]{:S(2)}) copy-start(f32[10,64,64]{2,1,0:T(8,128)} %param.22) | copy-start | bytes 491524
  13.0 139.4 %all-to-all-start = ((s32[128,1,3]{2,1,0:T(1,128)}), s32[128,1,3]{2,1,0:T(1,128)S(1)}, u32[]{:S(2)}, u32[]{:S(2)}) async-start(s32[128,1,3]{2,1,0:T(1,128)} %bitcast.4), calls=%async_computation | async-start | bytes 131072 | tf_op jit(solution)/shard_map/all_to_all | solution.py:95
  47.2 2.0 copy-start.8
  47.2 2.0 copy-start.7
  47.2 2.1 copy-start.6
  118.9 3.7 %copy-start.2 = (f32[128,64,32]{1,2,0:T(8,128)S(1)}, f32[128,64,32]{1,2,0:T(8,128)}, u32[]{:S(2)}) copy-start(f32[128,64,32]{1,2,0:T(8,128)} %gather_fusion.5) | copy-start | bytes 3145732
  152.5 116.6 %all-to-all-start.1 = ((f32[128,3,4096]{2,1,0:T(4,128)}), f32[128,3,4096]{2,1,0:T(4,128)}, u32[]{:S(2)}, u32[]{:S(2)}) async-start(f32[128,3,4096]{2,1,0:T(4,128)} %copy.103), calls=%async_computation.1 | async-start | bytes 16777216 | tf_op jit(solution)/shard_map/all_to_all | solution.py:88
  295.7 5.3 %copy-start.1 = (s32[16384]{0:T(1024)S(1)}, s32[16384]{0:T(1024)}, u32[]{:S(2)}) copy-start(s32[16384]{0:T(1024)} %param.20) | copy-start | bytes 196612
Sparse Core Ops, SparseCore 0:
  9.0 33.6 all-gather.4
  44.4 35.4 all-gather.2
where the time goes:
time: 309 us; the launch traced here: 308 us
  waiting for transfers between devices  130 us (42%)
  local copies, waits for them, and re-layouts  80.1 us (26%)
  matrix products  30.7 us (10%)
  blocking collectives  22.8 us (7%)
  starting transfers between devices  19.1 us (6%)
  between operations  13.8 us (4%)
  other arithmetic  11.2 us (4%)
    all_to_all x1, waiting for transfers between devices, body(): lax.all_to_all(outgoing.reshape(owners, capacity, flat_width), ('inst', '...  106 us
    all_gather x1, blocking collectives, body(): lax.all_gather(bubble_inverse, 'arch', axis=0, tiled=True)  22.8 us
    all_gather x1, waiting for transfers between devices, body(): lax.all_gather(port_stiffness, 'arch', axis=0, tiled=True)  22.4 us
    slice x5, local copies, waits for them, and re-layouts, body(): schur[:, which * width:(which + 1) * width, :][:, :, columns[which]]  13.4 us
    gather x4, local copies, waits for them, and re-layouts, body(): schur[:, which * width:(which + 1) * width, :][:, :, columns[which]]  13 us
    dot_general x1, matrix products, condense(): jnp.einsum('bmp,bmq->bpq', weighted, applied, precision=lax.Precision.HIG...  11.6 us
    all_to_all x1, starting transfers between devices, body(): lax.all_to_all(out_codes.reshape(owners, capacity), ('inst', 'arch'), spl...  10.5 us
    reshape x1, local copies, waits for them, and re-layouts, body(): incoming = incoming.reshape(owners * capacity, flat_width)  9.5 us
  transfers between devices with their start and end apart: 4, of which 2 were waited for; matrix products, arithmetic and copies ran while one was open for 29% of the time, Pallas kernels for 0%

commit v1 on v0

v1 whole, which is shorter than its diff:
```python
import functools

import jax
import jax.numpy as jnp
from jax import lax
from jax.experimental import pallas as pl
from jax.experimental.pallas import tpu as pltpu
from jax.sharding import PartitionSpec as P

MESH = pl.DeviceIdType.MESH
SIDE = 4
OFFSETS = (1, 3, 2)
LANES = 128
VMEM_LIMIT = 56 << 20


def position():
    inst, z = lax.axis_index("inst"), lax.axis_index("arch")
    return inst // (2 * SIDE), inst // 2 % SIDE, inst % 2, z


def device(x, y, core, z):
    return ((x * SIDE + y) * 2 + core, z)


def moved(here, axis, offset):
    there = list(here)
    there[axis] = (there[axis] + offset) % SIDE
    return tuple(there)


def greet(partners):
    barrier = pltpu.get_barrier_semaphore()
    for partner in partners:
        pl.semaphore_signal(barrier, inc=1, device_id=device(*partner), device_id_type=MESH)
    pl.semaphore_wait(barrier, len(partners))


def send(src, dst, send_sem, recv_sem, there):
    copy = pltpu.make_async_remote_copy(
        src, dst, send_sem, recv_sem, device_id=device(*there), device_id_type=MESH
    )
    copy.start()
    return copy


def take(ref, sem):
    pltpu.make_async_copy(ref, ref, sem).wait()


def gather_kernel(inverse, coupling, stiffness, basis, stiff, local, s1, r1, s2, r2, s3, r3):
    here = position()
    x, y, core, z = here
    other = (x, y, 1 - core, z)
    lines = [[moved(here, axis, o) for o in OFFSETS] for axis in (0, 1, 3)]
    greet([*lines[0], *lines[1], *lines[2], other])
    inverse_rows, basis_rows, stiff_rows = inverse.shape[0], basis.shape[1], stiff.shape[1]
    own = [
        pltpu.make_async_copy(inverse, basis.at[z, pl.ds(0, inverse_rows)], local.at[0]),
        pltpu.make_async_copy(
            coupling, basis.at[z, pl.ds(inverse_rows, basis_rows - inverse_rows)], local.at[1]
        ),
        pltpu.make_async_copy(stiffness, stiff.at[z], local.at[2]),
    ]
    for copy in own:
        copy.start()
    arrays = ((basis, (64, 56)), (stiff, (80, 80)))
    assert basis_rows == 8 * 120 and stiff_rows == 8 * 160

    def piece(ref, sizes, half, plane):
        size, base = sizes[half], half * 8 * sizes[0]
        return ref.at[plane, pl.ds(base + (core * SIDE + here[half]) * size, size)]

    def core_half(ref, sizes, half, plane, which):
        size, base = sizes[half], half * 8 * sizes[0]
        return ref.at[plane, pl.ds(base + which * SIDE * size, SIDE * size)]

    sent = []
    for a, (ref, sizes) in enumerate(arrays):
        for copy in own[:2] if a == 0 else own[2:]:
            copy.wait()
        for o, there in enumerate(lines[2]):
            for half in (0, 1):
                mine = piece(ref, sizes, half, z)
                sent.append(send(mine, mine, s1.at[a, o, half], r1.at[a, o, half], there))
    for a, (ref, sizes) in enumerate(arrays):
        for o, offset in enumerate(OFFSETS):
            plane = (z + SIDE - offset) % SIDE
            for half in (0, 1):
                got = piece(ref, sizes, half, plane)
                take(got, r1.at[a, o, half])
                for i, there in enumerate(lines[half]):
                    sent.append(send(got, got, s2.at[a, o, half, i], r2.at[a, o, half, i], there))
    for a, (ref, sizes) in enumerate(arrays):
        for o, offset in enumerate(OFFSETS):
            plane = (z + SIDE - offset) % SIDE
            for half in (0, 1):
                for i in range(3):
                    take(piece(ref, sizes, half, plane), r2.at[a, o, half, i])
                got = core_half(ref, sizes, half, plane, core)
                sent.append(send(got, got, s3.at[a, o, half], r3.at[a, o, half], other))
    for a, (ref, sizes) in enumerate(arrays):
        for o, offset in enumerate(OFFSETS):
            plane = (z + SIDE - offset) % SIDE
            for half in (0, 1):
                take(core_half(ref, sizes, half, plane, 1 - core), r3.at[a, o, half])
    for copy in sent:
        copy.wait_send()


def gather_bases(inverse, coupling, stiffness):
    dma = pltpu.SemaphoreType.DMA
    rows = inverse.shape[0] + coupling.shape[0]
    return pl.pallas_call(
        gather_kernel,
        out_shape=(
            jax.ShapeDtypeStruct((SIDE, rows, LANES), jnp.float32),
            jax.ShapeDtypeStruct((SIDE, stiffness.shape[0], LANES), jnp.float32),
        ),
        in_specs=[pl.BlockSpec(memory_space=pl.ANY)] * 3,
        out_specs=[pl.BlockSpec(memory_space=pl.ANY)] * 2,
        scratch_shapes=[
            dma((3,)),
            dma((2, 3, 2)),
            dma((2, 3, 2)),
            dma((2, 3, 2, 3)),
            dma((2, 3, 2, 3)),
            dma((2, 3, 2)),
            dma((2, 3, 2)),
        ],
        compiler_params=pltpu.CompilerParams(
            collective_id=0, has_side_effects=True, vmem_limit_bytes=VMEM_LIMIT
        ),
        name="gather_bases",
    )(inverse, coupling, stiffness)


def halves(value):
    high = value.astype(jnp.bfloat16).astype(jnp.float32)
    return high, value - high


def condense_kernel(arch, basis, stiff, scales, offset, strips, table):
    step = pl.program_id(0)
    block, modes = offset.shape[0], offset.shape[1]
    archs = stiff.shape[1] // LANES
    half = modes // 2
    lane = lax.broadcasted_iota(jnp.int32, (LANES, LANES), 1)
    left = lane < modes

    @pl.when(step == 0)
    def _():
        def one(a, carry):
            plane, at = a // archs, a % archs
            packed = basis[plane, pl.ds(pl.multiple_of(at * half, half), half), :]
            turned = pltpu.roll(packed, modes, 1)
            left_half = left[:half]
            both = jnp.concatenate(
                [jnp.where(left_half, packed, turned), jnp.where(left_half, turned, packed)], axis=0
            )
            high, low = halves(both)
            table[a] = jnp.concatenate([high, high, low, low], axis=0).astype(jnp.bfloat16)
            return carry

        lax.fori_loop(0, SIDE * archs, one, 0)

    lane8 = lane[: LANES // 4]
    for u in range(block):
        a = arch[step * block + u]
        plane, at = a // archs, a % archs
        start = pl.multiple_of(archs * half + at * modes, half)
        body = basis[plane, pl.ds(start, modes), :] + offset[u]
        weighted = jnp.concatenate([body, body], axis=0).T * scales[u : u + 1, :]
        high, low = halves(weighted)
        mixed = jnp.where(left, weighted, low).astype(jnp.bfloat16)
        applied = jnp.dot(
            jnp.concatenate([mixed, mixed], axis=1), table[a], preferred_element_type=jnp.float32
        )
        rest = halves(applied)[1]
        mixed = jnp.where(left, applied, rest).astype(jnp.bfloat16)
        product = lax.dot_general(
            jnp.concatenate([mixed, mixed], axis=1),
            jnp.concatenate([high.astype(jnp.bfloat16), low.astype(jnp.bfloat16)], axis=1),
            (((1,), (1,)), ((), ())),
            preferred_element_type=jnp.float32,
        )
        schur = stiff[plane, pl.ds(pl.multiple_of(at * LANES, LANES), LANES), :] - product
        for k in range(4):
            v = schur[k * 32 : (k + 1) * 32]
            if k > 0:
                first = pltpu.roll(v, LANES - 32 * k, 1)
                after = pltpu.roll(v, 32, 1)
                v = jnp.where(lane8 < 32, first, jnp.where(lane8 < 32 * (k + 1), after, v))
            strips[u, k] = v


def condense(arch, basis, stiff, scales, offset):
    block = 8
    instances, modes = offset.shape[0], offset.shape[1]
    count = SIDE * stiff.shape[1] // LANES
    return pl.pallas_call(
        condense_kernel,
        out_shape=jax.ShapeDtypeStruct((instances, 4, 32, LANES), jnp.float32),
        grid_spec=pltpu.PrefetchScalarGridSpec(
            num_scalar_prefetch=1,
            grid=(instances // block,),
            in_specs=[
                pl.BlockSpec(basis.shape, lambda i, a: (0, 0, 0), pipeline_mode=pl.Buffered(1)),
                pl.BlockSpec(stiff.shape, lambda i, a: (0, 0, 0), pipeline_mode=pl.Buffered(1)),
                pl.BlockSpec((block, LANES), lambda i, a: (i, 0)),
                pl.BlockSpec((block, modes, LANES), lambda i, a: (i, 0, 0)),
            ],
            out_specs=pl.BlockSpec((block, 4, 32, LANES), lambda i, a: (i, 0, 0, 0)),
            scratch_shapes=[pltpu.VMEM((count, 4 * modes, LANES), jnp.bfloat16)],
        ),
        compiler_params=pltpu.CompilerParams(vmem_limit_bytes=VMEM_LIMIT),
        name="condense",
    )(arch, basis, stiff, scales, offset)


ORDERS = ((0, 1, 3), (1, 3, 0), (3, 0, 1))


def exchange_kernel(slot_strip, slot_code, strips, arrived, first, second, third, local, ss, rs):
    here = position()
    core = here[2]
    other = (here[0], here[1], 1 - core, here[3])
    partners = [other]
    for axis in (0, 1, 3):
        for o in OFFSETS:
            there = moved(here, axis, o)
            partners += [there, (there[0], there[1], 1 - core, there[3])]
    greet(partners)
    row = lax.broadcasted_iota(jnp.int32, (8, LANES), 0)
    lane = lax.broadcasted_iota(jnp.int32, (8, LANES), 1)
    spot = (row == 1) & (lane == 0)

    def pack(part, line, into):
        def one(i, carry):
            at = part * 128 + line * 32 + i
            which = slot_strip[at]
            into[i // 8, i % 8, 8:] = strips[which, 8:]
            into[i // 8, i % 8, :8] = jnp.where(spot, slot_code[at], strips[which, :8])
            return carry

        lax.fori_loop(0, 32, one, 0, unroll=4)

    sent, copies = [], []
    for i, o in enumerate(OFFSETS):
        for part, (a1, a2, a3) in enumerate(ORDERS):
            line = (here[a1] + o) % SIDE
            pack(part, line, first.at[part, line])
            sent.append(
                send(
                    first.at[part, line],
                    second.at[part, here[a1]],
                    ss.at[part, 0, i],
                    rs.at[part, 0, i],
                    moved(here, a1, o),
                )
            )
    for part, (a1, a2, a3) in enumerate(ORDERS):
        pack(part, here[a1], second.at[part, here[a1]])
    for part, (a1, a2, a3) in enumerate(ORDERS):
        for i, o in enumerate(OFFSETS):
            take(second.at[part, 0], rs.at[part, 0, i])
        for i, o in enumerate(OFFSETS):
            line = (here[a2] + o) % SIDE
            sent.append(
                send(
                    second.at[part, :, line],
                    third.at[part, here[a2]],
                    ss.at[part, 1, i],
                    rs.at[part, 1, i],
                    moved(here, a2, o),
                )
            )
        copy = pltpu.make_async_copy(
            second.at[part, :, here[a2]], third.at[part, here[a2]], local.at[part, 0]
        )
        copy.start()
        copies.append(copy)
    for part, (a1, a2, a3) in enumerate(ORDERS):
        copies[part].wait()
        for i, o in enumerate(OFFSETS):
            take(third.at[part, 0], rs.at[part, 1, i])
        mine = here[a3] * 2 + core
        n = 2
        for o in (*OFFSETS, 0):
            for flip in (0, 1):
                there = moved(here, a3, o)
                to = (core + flip) % 2
                there = (there[0], there[1], to, there[3])
                src = third.at[part, :, :, there[a3] * 2 + to]
                dst = arrived.at[part, mine]
                if o == 0 and flip == 0:
                    copy = pltpu.make_async_copy(src, dst, local.at[part, 1])
                    copy.start()
                    copies.append(copy)
                else:
                    sent.append(send(src, dst, ss.at[part, 2, n - 2], rs.at[part, 2, n - 2], there))
                    n += 1
    for part in range(3):
        copies[3 + part].wait()
        for i in range(7):
            take(arrived.at[part, 0], rs.at[part, 2, i])
    for copy in sent:
        copy.wait_send()


def exchange(slot_strip, slot_code, strips):
    dma = pltpu.SemaphoreType.DMA
    return pl.pallas_call(
        exchange_kernel,
        out_shape=jax.ShapeDtypeStruct((3, 2 * SIDE, SIDE, SIDE, 32, LANES), jnp.float32),
        in_specs=[
            pl.BlockSpec(memory_space=pltpu.SMEM),
            pl.BlockSpec(memory_space=pltpu.SMEM),
            pl.BlockSpec(memory_space=pltpu.VMEM),
        ],
        out_specs=pl.BlockSpec(memory_space=pl.ANY),
        scratch_shapes=[
            pltpu.VMEM((3, SIDE, SIDE, 8, 32, LANES), jnp.float32),
            pltpu.VMEM((3, SIDE, SIDE, 8, 32, LANES), jnp.float32),
            pltpu.VMEM((3, SIDE, SIDE, 8, 32, LANES), jnp.float32),
            dma((3, 2)),
            dma((3, 3, 7)),
            dma((3, 3, 7)),
        ],
        compiler_params=pltpu.CompilerParams(
            collective_id=1, has_side_effects=True, vmem_limit_bytes=VMEM_LIMIT
        ),
        name="exchange",
    )(slot_strip, slot_code, strips)


def assemble_kernel(where, arrived, out, even, odd, sems):
    step, steps = pl.program_id(0), pl.num_programs(0)

    def copies(at, slot):
        for r in range(8):
            for parity, buffer in enumerate((even, odd)):
                yield pltpu.make_async_copy(
                    arrived.at[where[(at * 8 + r) * 2 + parity]],
                    buffer.at[slot, pl.ds(r * 32, 32)],
                    sems.at[slot, parity, r],
                )

    @pl.when(step == 0)
    def _():
        for copy in copies(0, 0):
            copy.start()

    @pl.when(step + 1 < steps)
    def _():
        for copy in copies(step + 1, (step + 1) % 2):
            copy.start()

    slot = step % 2
    for copy in copies(step, slot):
        copy.wait()
    lane = lax.broadcasted_iota(jnp.int32, (8, LANES), 1)

    def row(i):
        e = even[slot, pl.ds(i, 8, stride=32), :]
        o = odd[slot, pl.ds(i, 8, stride=32), :]
        return jnp.where(lane < 32, e + o, e), o

    for g in range(8):
        (s0, o0), (s1, o1), (s2, o2), (s3, o3) = (row(4 * g + i) for i in range(4))
        if g == 0:
            s1 = jnp.where(lane == 0, pltpu.roll(s0, LANES - 1, 1), s1)
        tiles = (
            s0,
            pltpu.roll(jnp.where(lane < 32, s1, o0), 96, 1),
            jnp.where(lane < 96, pltpu.roll(s1, 96, 1), pltpu.roll(o1, 64, 1)),
            pltpu.roll(jnp.where(lane < 64, s2, o1), 64, 1),
            jnp.where(lane < 64, pltpu.roll(s2, 64, 1), pltpu.roll(o2, 32, 1)),
            pltpu.roll(jnp.where(lane < 96, s3, o2), 32, 1),
            jnp.where(lane < 32, pltpu.roll(s3, 32, 1), o3),
        )
        for t, tile in enumerate(tiles):
            out[:, (7 * g + t) * LANES : (7 * g + t + 1) * LANES] = tile


def assemble(where, arrived, ports):
    return pl.pallas_call(
        assemble_kernel,
        out_shape=jax.ShapeDtypeStruct((ports, 56 * LANES), jnp.float32),
        grid_spec=pltpu.PrefetchScalarGridSpec(
            num_scalar_prefetch=1,
            grid=(ports // 8,),
            in_specs=[pl.BlockSpec(memory_space=pl.ANY)],
            out_specs=pl.BlockSpec((8, 56 * LANES), lambda i, w: (i, 0)),
            scratch_shapes=[
                pltpu.VMEM((2, 8 * 32, LANES), jnp.float32),
                pltpu.VMEM((2, 8 * 32, LANES), jnp.float32),
                pltpu.SemaphoreType.DMA((2, 2, 8)),
            ],
        ),
        compiler_params=pltpu.CompilerParams(vmem_limit_bytes=VMEM_LIMIT),
        name="assemble",
    )(where, arrived)


def body(
    instance_arch,
    instance_param,
    instance_ports,
    port_row,
    param_table,
    bubble_inverse,
    coupling,
    port_stiffness,
    coupling_offset,
):
    instances = instance_arch.shape[0]
    ports = 2 * instances
    archs, modes = bubble_inverse.shape[:2]
    packed = jnp.concatenate(
        [bubble_inverse[:, : modes // 2], bubble_inverse[:, modes // 2 :]], axis=2
    )
    basis, stiff = gather_bases(
        packed.reshape(archs * modes // 2, LANES),
        coupling.reshape(archs * modes, LANES),
        port_stiffness.reshape(archs * LANES, LANES),
    )
    scales = jnp.take(param_table, instance_param, axis=0)
    scales = jnp.concatenate([scales, scales], axis=1)

    count = 4 * instances
    strip = jnp.arange(count, dtype=jnp.int32)
    rows = jnp.take(port_row, instance_ports.reshape(count), axis=0)
    owner = rows // ports
    code = rows % ports * 2 + strip % 2
    earlier = (owner[:, None] == owner[None, :]) & (strip[None, :] < strip[:, None])
    ordinal = jnp.sum(earlier.astype(jnp.int32), axis=1)
    z, core, y, x = owner % 4, owner // 4 % 2, owner // 8 % 4, owner // 32
    place = jnp.where(
        ordinal == 0,
        (x * 4 + y) * 8 + z * 2 + core,
        jnp.where(ordinal == 1, 128 + (y * 4 + z) * 8 + x * 2 + core, 256 + (z * 4 + x) * 8 + y * 2 + core),
    )
    slots = jnp.arange(384, dtype=jnp.int32)
    chosen = place[None, :] == slots[:, None]
    slot_strip = jnp.sum(jnp.where(chosen, strip[None, :], 0), axis=1)
    slot_code = jnp.sum(jnp.where(chosen, code[None, :] + 1, 0), axis=1).astype(jnp.float32) - 1.0

    strips = condense(instance_arch, basis, stiff, scales, coupling_offset)
    arrived = exchange(slot_strip, slot_code, strips.reshape(count, 32, LANES))
    arrived = arrived.reshape(384, 32, LANES)
    codes = arrived[:, 1, 0]
    wanted = jnp.arange(2 * ports, dtype=jnp.int32).astype(jnp.float32)
    where = jnp.sum(jnp.where(codes[None, :] == wanted[:, None], slots[None, :], 0), axis=1)
    return assemble(where, arrived, ports)


def solution(mesh):
    return jax.shard_map(
        body,
        mesh=mesh,
        in_specs=(
            P(("inst", "arch")),
            P(("inst", "arch")),
            P(("inst", "arch"), None),
            P(),
            P(),
            P("arch", None, None),
            P("arch", None, None),
            P("arch", None, None),
            P(("inst", "arch"), None, None),
        ),
        out_specs=P(("inst", "arch"), None),
        check_vma=False,
    )
```

time: 309 us -> 177 us (0.57)
  the two profiles are of different devices: /device:TPU:6 before, /device:TPU:1 now
where the time goes in v1:
time: 177 us; the launch traced here: 176 us
  Pallas kernels  165 us (93%)
  local copies, waits for them, and re-layouts  7.01 us (4%)
  other arithmetic  3.82 us (2%)
    pallas_call x1, Pallas kernels, exchange(): pl.pallas_call(exchange_kernel, out_shape=jax.ShapeDtypeStruct((3, 2 * SI...  80.2 us
    pallas_call x1, Pallas kernels, gather_bases(): pl.pallas_call(gather_kernel, out_shape=(jax.ShapeDtypeStruct((SIDE, rows...  58.7 us
    pallas_call x1, Pallas kernels, condense(): pl.pallas_call(condense_kernel, out_shape=jax.ShapeDtypeStruct((instances...  13.9 us
    pallas_call x1, Pallas kernels, assemble(): pl.pallas_call(assemble_kernel, out_shape=jax.ShapeDtypeStruct((ports, 56...  11.9 us

profile of v1, /device:TPU:1, one launch (start us, length us, event | category | flops | bytes accessed | tf_op | source)
XLA Modules:
  0.0 175.7 jit_solution(14656815267691220733)
XLA Ops:
  0.0 0.0 copy-start
  0.0 0.0 copy-start.1
  0.0 0.0 copy-start.2
  0.0 0.8 copy.14
  0.8 0.1 reshape.263
  1.0 0.0 copy-done
  1.0 1.7 gather_fusion
  2.7 0.1 reshape.262
  2.8 0.2 convert_reduce_fusion
  3.0 0.8 select_reduce_fusion.1
  3.8 0.5 convert_add_fusion.slot_code
  4.4 1.0 fusion.6
  5.4 0.8 pad_maximum_fusion
  6.2 58.7 %gather_bases.1 = (f32[4,960,128]{2,1,0:T(8,128)}, f32[4,1280,128]{2,1,0:T(8,128)}) custom-call(f32[320,128]{1,0:T(8,128)} %bitcast.10, f32[640,128]{1,0:T(8,128)} %bitcast.11, f32[1280,128]{1,0:T(8,128)} %bitcast.9), custom_call_target="tpu_custom_call" | custom-call | tf_op jit(solution)/shard_map/gather_bases/pallas_call | solution.py:114
  64.9 0.0 copy-done.1
  64.9 0.2 copy.16
  65.1 0.0 copy-done.2
  65.1 0.6 gather_fusion.1
  65.8 0.1 broadcast_select_fusion
  65.8 0.7 pad_maximum_fusion.1.scales
  66.5 13.9 %condense.1 = f32[64,4,32,128]{3,2,1,0:T(8,128)} custom-call(s32[64]{0:T(128)} %arch.1, f32[4,960,128]{2,1,0:T(8,128)} %get-tuple-element.7.basis, f32[4,1280,128]{2,1,0:T(8,128)} %get-tuple-element.8.stiff, f32[64,128]{1,0:T(8,128)} %pad_maximum_fusion.1.scales, f32[64,64,128]{2,1,0:T(8,128)} %offset.1), custom_call_target="tpu_custom_call" | custom-call | tf_op jit(solution)/shard_map/condense/pallas_call | solution.py:201
  80.5 80.2 %exchange.1 = f32[3,8,4,4,32,128]{5,4,3,2,1,0:T(8,128)} custom-call(s32[384]{0:T(512)} %get-tuple-element.10.slot_strip, f32[384]{0:T(512)} %convert_add_fusion.slot_code, f32[256,32,128]{2,1,0:T(8,128)} %bitcast.8), custom_call_target="tpu_custom_call" | custom-call | tf_op jit(solution)/shard_map/exchange/pallas_call | solution.py:313
  160.7 2.4 %slice_reduce_fusion = f32[384]{0:T(512)S(1)} fusion(f32[384,32,128]{2,1,0:T(8,128)} %bitcast.6), kind=kLoop, calls=%fused_computation.9 | loop fusion | bytes 3072 | tf_op jit(solution)/shard_map/slice | solution.py:452
  163.1 0.7 select_reduce_fusion.where
  163.8 11.9 %assemble.1 = f32[128,7168]{1,0:T(8,128)} custom-call(s32[256]{0:T(256)} %select_reduce_fusion.where, f32[384,32,128]{2,1,0:T(8,128)} %bitcast.7), custom_call_target="tpu_custom_call" | custom-call | tf_op jit(solution)/shard_map/assemble/pallas_call | solution.py:387
  (8 shorter events, 0.1 us)
Async XLA Ops:
  0.0 1.0 copy-start
  0.0 64.9 %copy-start.1 = (f32[1024,64]{0,1:T(8,128)S(1)}, f32[1024,64]{0,1:T(8,128)}, u32[]{:S(2)}) copy-start(f32[1024,64]{0,1:T(8,128)} %param.13) | copy-start | bytes 786436
  0.0 65.1 %copy-start.2 = (s32[64]{0:T(128)S(1)}, s32[64]{0:T(128)}, u32[]{:S(2)}) copy-start(s32[64]{0:T(128)} %param.10) | copy-start | bytes 772

commit v2 on v1

v2 whole, which is shorter than its diff:
```python
import functools

import jax
import jax.numpy as jnp
from jax import lax
from jax.experimental import pallas as pl
from jax.experimental.pallas import tpu as pltpu
from jax.sharding import PartitionSpec as P

MESH = pl.DeviceIdType.MESH
SIDE = 4
OFFSETS = (1, 3, 2)
LANES = 128
VMEM_LIMIT = 56 << 20


def position():
    inst, z = lax.axis_index("inst"), lax.axis_index("arch")
    return inst // (2 * SIDE), inst // 2 % SIDE, inst % 2, z


def device(x, y, core, z):
    return ((x * SIDE + y) * 2 + core, z)


def moved(here, axis, offset):
    there = list(here)
    there[axis] = (there[axis] + offset) % SIDE
    return tuple(there)


def greet(partners):
    barrier = pltpu.get_barrier_semaphore()
    for partner in partners:
        pl.semaphore_signal(barrier, inc=1, device_id=device(*partner), device_id_type=MESH)
    pl.semaphore_wait(barrier, len(partners))


def send(src, dst, send_sem, recv_sem, there):
    copy = pltpu.make_async_remote_copy(
        src, dst, send_sem, recv_sem, device_id=device(*there), device_id_type=MESH
    )
    copy.start()
    return copy


def take(ref, sem):
    pltpu.make_async_copy(ref, ref, sem).wait()


PIECES = ((64, 56), (80, 80))
ORDERS = ((0, 1, 3), (1, 3, 0), (3, 0, 1))


def halves(value):
    high = value.astype(jnp.bfloat16).astype(jnp.float32)
    return high, value - high


def reorder(v, k):
    if k == 0:
        return v
    lane = lax.broadcasted_iota(jnp.int32, v.shape, 1)
    first = pltpu.roll(v, LANES - 32 * k, 1)
    after = pltpu.roll(v, 32, 1)
    return jnp.where(lane < 32, first, jnp.where(lane < 32 * (k + 1), after, v))


def strips_kernel(
    arch,
    param,
    ports,
    row_in,
    params_in,
    inverse_in,
    coupling_in,
    stiffness_in,
    offset_in,
    arrived_out,
    where,
    arrived,
    inverse,
    basis,
    stiff,
    offset,
    turned,
    inverse_table,
    natural,
    coupling_table,
    stiff_table,
    strips,
    scales,
    params,
    rows,
    slots_vector,
    slots,
    first,
    second,
    third,
    local,
    s1,
    r1,
    s2,
    r2,
    s3,
    r3,
    here_sems,
    out_sems,
    ss,
    rs,
):
    here = position()
    x, y, core, z = here
    other = (x, y, 1 - core, z)
    lines = {axis: [moved(here, axis, o) for o in OFFSETS] for axis in (0, 1, 3)}
    archs, modes = inverse.shape[0], inverse.shape[1]
    instances = offset.shape[0]
    half_modes = modes // 2
    inverse_rows, coupling_rows = archs * half_modes, archs * modes
    own = [
        pltpu.make_async_copy(inverse_in, inverse, local.at[0]),
        pltpu.make_async_copy(coupling_in, basis.at[z, pl.ds(inverse_rows, coupling_rows)], local.at[1]),
        pltpu.make_async_copy(stiffness_in, stiff.at[z], local.at[2]),
        pltpu.make_async_copy(offset_in, offset, local.at[3]),
        pltpu.make_async_copy(row_in, rows, local.at[4]),
        pltpu.make_async_copy(params_in, params, local.at[5]),
    ]
    for copy in own:
        copy.start()
    partners = [other]
    for axis in (0, 1, 3):
        for there in lines[axis]:
            partners += [there, (there[0], there[1], 1 - core, there[3])]
    greet(partners)

    lane = lax.broadcasted_iota(jnp.int32, (LANES, LANES), 1)
    left = lane < modes
    left_half = left[:half_modes]
    row8 = lax.broadcasted_iota(jnp.int32, (8, LANES), 0)
    lane8 = lane[:8]

    own[0].wait()
    for a in range(archs):
        top = jnp.concatenate([inverse[a, :half_modes], inverse[a, half_modes:]], axis=1)
        basis[z, a * half_modes : (a + 1) * half_modes] = top
    own[1].wait()
    arrays = ((basis, PIECES[0]), (stiff, PIECES[1]))

    def piece(a, half, plane):
        ref, sizes = arrays[a]
        size, base = sizes[half], half * 8 * sizes[0]
        return ref.at[plane, pl.ds(base + (core * SIDE + here[half]) * size, size)]

    def core_half(a, half, plane, which):
        ref, sizes = arrays[a]
        size, base = sizes[half], half * 8 * sizes[0]
        return ref.at[plane, pl.ds(base + which * SIDE * size, SIDE * size)]

    sent = []
    planes = [(z + SIDE - o) % SIDE for o in OFFSETS]

    def along_z(a):
        for o, there in enumerate(lines[3]):
            for half in (0, 1):
                mine = piece(a, half, z)
                sent.append(send(mine, mine, s1.at[a, o, half], r1.at[a, o, half], there))

    def along_lines(a):
        for o, plane in enumerate(planes):
            for half in (0, 1):
                got = piece(a, half, plane)
                take(got, r1.at[a, o, half])
                for i, there in enumerate(lines[half]):
                    sent.append(send(got, got, s2.at[a, o, half, i], r2.at[a, o, half, i], there))

    def to_other_core(a):
        for o, plane in enumerate(planes):
            for half in (0, 1):
                for i in range(3):
                    take(piece(a, half, plane), r2.at[a, o, half, i])
                got = core_half(a, half, plane, core)
                sent.append(send(got, got, s3.at[a, o, half], r3.at[a, o, half], other))

    def wait_plane(a, o):
        for half in (0, 1):
            take(core_half(a, half, planes[o], 1 - core), r3.at[a, o, half])

    def basis_tables(plane):
        def one(at, carry):
            packed = basis[plane, pl.ds(pl.multiple_of(at * half_modes, half_modes), half_modes), :]
            flipped = pltpu.roll(packed, modes, 1)
            both = jnp.concatenate(
                [jnp.where(left_half, packed, flipped), jnp.where(left_half, flipped, packed)], axis=0
            )
            high, low = halves(both)
            inverse_table[plane * archs + at] = jnp.concatenate([high, high, low, low], axis=0).astype(
                jnp.bfloat16
            )
            begin = pl.multiple_of(inverse_rows + at * modes, half_modes)
            c = basis[plane, pl.ds(begin, modes), :]
            natural[plane * archs + at] = c
            coupling_table[plane * archs + at] = jnp.concatenate([c, c], axis=0).T
            return carry

        lax.fori_loop(0, archs, one, 0, unroll=2)

    def stiff_tables(plane):
        def one(at, carry):
            for k in range(4):
                begin = pl.multiple_of(at * LANES + k * 32, 32)
                stiff_table[(plane * archs + at) * 4 + k] = reorder(stiff[plane, pl.ds(begin, 32), :], k)
            return carry

        lax.fori_loop(0, archs, one, 0)

    def turn(begin, end):
        def one(i, carry):
            v = offset[i]
            turned[i] = jnp.concatenate([v, v], axis=0).T
            return carry

        lax.fori_loop(begin, end, one, 0, unroll=2)

    def look_up_scales():
        wanted = jnp.zeros((8, LANES), jnp.int32)
        for i in range(instances):
            wanted = jnp.where(lane8 == i, param[i], wanted)
        samples = params.shape[1]
        sample = lax.broadcasted_iota(jnp.int32, (samples, LANES), 0)
        chosen = jnp.where(sample == wanted[:1], 1.0, 0.0).astype(jnp.bfloat16)
        high, rest = halves(params[...])
        middle, low = halves(rest)
        found = jnp.zeros((modes, LANES), jnp.float32)
        for part in (high, middle, low):
            found = found + jnp.dot(part.astype(jnp.bfloat16), chosen, preferred_element_type=jnp.float32)
        scales[...] = jnp.concatenate([found, found], axis=0).T[:instances]

    def place_strips():
        def one(i, carry):
            low, high = carry
            low = jnp.where(lane8 == i, rows[ports[0, i]], low)
            low = jnp.where(lane8 == i + instances, rows[ports[1, i]], low)
            high = jnp.where(lane8 == i, rows[ports[2, i]], high)
            high = jnp.where(lane8 == i + instances, rows[ports[3, i]], high)
            return low, high

        zero = jnp.zeros((8, LANES), jnp.int32)
        row = lax.fori_loop(0, instances, one, (zero, zero), unroll=8)

        def down(v):
            return jnp.broadcast_to(v[:1], (LANES, LANES)).T

        wanted = jnp.zeros((8, LANES), jnp.int32)
        for i in range(instances):
            wanted = jnp.where((lane8 == i) | (lane8 == i + instances), arch[i] * 4, wanted)
        sub = lax.broadcasted_iota(jnp.int32, (LANES, LANES), 0)
        owner = [v >> 7 for v in row]
        owner_down = [down(v) for v in owner]
        places, values = [], []
        for h in (0, 1):
            across = owner[h][:1]
            same = jnp.where((owner_down[h] == across) & (sub < lane), 1, 0)
            if h == 1:
                same = same + jnp.where(owner_down[0] == across, 1, 0)
            ordinal = jnp.sum(same, axis=0, keepdims=True)
            oz, oc, oy, ox = across & 3, (across >> 2) & 1, (across >> 3) & 3, across >> 5
            place = jnp.where(
                ordinal == 0,
                (ox * 4 + oy) * 8 + oz * 2 + oc,
                jnp.where(
                    ordinal == 1,
                    128 + (oy * 4 + oz) * 8 + ox * 2 + oc,
                    256 + (oz * 4 + ox) * 8 + oy * 2 + oc,
                ),
            )
            odd = jnp.where(lane8[:1] < instances, 0, 1)
            code = (row[h][:1] & 127) * 2 + odd
            stiff_at = wanted[:1] + odd + 2 * h
            places.append(down(place))
            values.append(down((stiff_at << 17) + ((code + 1) << 8) + lane8[:1] + h * LANES))
        for j in range(3):
            target = lane8[:1] + j * LANES
            total = jnp.zeros((LANES, LANES), jnp.int32)
            for h in (0, 1):
                total = jnp.maximum(total, jnp.where(places[h] == target, values[h], 0))
            value = jnp.max(total, axis=0, keepdims=True)
            slots_vector[j : j + 1] = value & 255
            slots_vector[j + 3 : j + 4] = ((value >> 8) & 511) - 1
            slots_vector[j + 6 : j + 7] = value >> 17

    along_z(0)
    own[2].wait()
    own[4].wait()
    place_strips()
    to_scalars = pltpu.make_async_copy(slots_vector, slots, local.at[6])
    to_scalars.start()
    along_lines(0)
    along_z(1)
    own[3].wait()
    own[5].wait()
    look_up_scales()
    basis_tables(z)
    to_other_core(0)
    turn(0, instances // 2)
    along_lines(1)
    turn(instances // 2, instances)
    stiff_tables(z)
    for o in range(3):
        wait_plane(0, o)
        basis_tables(planes[o])
    to_other_core(1)

    def condense(step, carry):
        for u in range(4):
            i = step * 4 + u
            a = arch[i]
            scale = scales[pl.ds(i, 1), :]
            weighted = (coupling_table[a] + turned[i]) * scale
            mixed = jnp.where(left, weighted, halves(weighted)[1]).astype(jnp.bfloat16)
            applied = scale * jnp.dot(
                jnp.concatenate([mixed, mixed], axis=1),
                inverse_table[a],
                preferred_element_type=jnp.float32,
            )
            mixed = jnp.where(left, applied, halves(applied)[1]).astype(jnp.bfloat16)
            high, low = halves(natural[a] + offset[i])
            product = jnp.dot(
                jnp.concatenate([mixed, mixed], axis=1),
                jnp.concatenate([high, high, low, low], axis=0).astype(jnp.bfloat16),
                preferred_element_type=jnp.float32,
            )
            for k in range(4):
                strips[k * instances + i] = reorder(product[k * 32 : (k + 1) * 32], k)
        return carry

    lax.fori_loop(0, instances // 4, condense, 0)
    for o in range(3):
        wait_plane(1, o)
        stiff_tables(planes[o])

    to_scalars.wait()
    spot = (row8 == 1) & (lane8 == 0)

    def pack(part, line, into):
        def one(i, carry):
            at = line * 32 + i
            strip = slots[part, at]
            stiff_at = slots[part + 6, at]
            into[i // 8, i % 8, 8:] = stiff_table[stiff_at, 8:] - strips[strip, 8:]
            top = stiff_table[stiff_at, :8] - strips[strip, :8]
            into[i // 8, i % 8, :8] = jnp.where(spot, slots[part + 3, at].astype(jnp.float32), top)
            return carry

        lax.fori_loop(0, 32, one, 0, unroll=4)

    copies = []
    for i, o in enumerate(OFFSETS):
        for part, (a1, a2, a3) in enumerate(ORDERS):
            line = (here[a1] + o) % SIDE
            pack(part, line, first.at[part, line])
            sent.append(
                send(
                    first.at[part, line],
                    second.at[part, here[a1]],
                    ss.at[part, 0, i],
                    rs.at[part, 0, i],
                    moved(here, a1, o),
                )
            )
    for part, (a1, a2, a3) in enumerate(ORDERS):
        pack(part, here[a1], second.at[part, here[a1]])
    for part, (a1, a2, a3) in enumerate(ORDERS):
        for i, o in enumerate(OFFSETS):
            take(second.at[part, 0], rs.at[part, 0, i])
        for i, o in enumerate(OFFSETS):
            line = (here[a2] + o) % SIDE
            sent.append(
                send(
                    second.at[part, :, line],
                    third.at[part, here[a2]],
                    ss.at[part, 1, i],
                    rs.at[part, 1, i],
                    moved(here, a2, o),
                )
            )
        copy = pltpu.make_async_copy(
            second.at[part, :, here[a2]], third.at[part, here[a2]], here_sems.at[part, 0]
        )
        copy.start()
        copies.append(copy)
    for part, (a1, a2, a3) in enumerate(ORDERS):
        copies[part].wait()
        for i, o in enumerate(OFFSETS):
            take(third.at[part, 0], rs.at[part, 1, i])
        mine = here[a3] * 2 + core
        n = 0
        for o in (*OFFSETS, 0):
            for flip in (0, 1):
                there = moved(here, a3, o)
                to = (core + flip) % 2
                there = (there[0], there[1], to, there[3])
                src = third.at[part, :, :, there[a3] * 2 + to]
                dst = arrived.at[part, mine]
                if o == 0 and flip == 0:
                    copy = pltpu.make_async_copy(src, dst, here_sems.at[part, 1])
                    copy.start()
                    copies.append(copy)
                else:
                    sent.append(send(src, dst, ss.at[part, 2, n], rs.at[part, 2, n], there))
                    n += 1
    out = []
    for part, (a1, a2, a3) in enumerate(ORDERS):
        mine = here[a3] * 2 + core
        n = 0
        for o in (0, *OFFSETS):
            for flip in (0, 1):
                origin = (here[a3] + SIDE - o) % SIDE * 2 + (core + flip) % 2
                if o == 0 and flip == 0:
                    copies[3 + part].wait()
                else:
                    take(arrived.at[part, origin], rs.at[part, 2, (n + 6) % 7])
                    n += 1
                copy = pltpu.make_async_copy(
                    arrived.at[part, origin], arrived_out.at[part, origin], out_sems.at[part, n]
                )
                copy.start()
                out.append(copy)
    landed = arrived.reshape(384 * 32, LANES)
    found = [jnp.zeros((8, LANES), jnp.int32)] * 2
    for g in range(48):
        codes = landed[pl.ds(g * 256 + 1, 8, stride=32), :][:, :1]
        for t in (0, 1):
            hit = codes == (lane8 + t * LANES).astype(jnp.float32)
            found[t] = found[t] + jnp.where(hit, row8 + g * 8, 0)
    for t in (0, 1):
        where[t : t + 1, :] = jnp.sum(found[t], axis=0, keepdims=True)
    for copy in sent:
        copy.wait_send()
    for copy in out:
        copy.wait()


def strips_of(arch, param, ports, rows, params, inverse, coupling, stiffness, offset):
    dma = pltpu.SemaphoreType.DMA
    archs, modes = inverse.shape[:2]
    instances, count = offset.shape[0], SIDE * archs
    f32 = jnp.float32
    assert archs * modes * 3 // 2 == 8 * sum(PIECES[0]) and archs * LANES == 8 * sum(PIECES[1])
    smem, vmem, anywhere = (
        pl.BlockSpec(memory_space=m) for m in (pltpu.SMEM, pltpu.VMEM, pl.ANY)
    )
    return pl.pallas_call(
        strips_kernel,
        out_shape=(
            jax.ShapeDtypeStruct((3, 2 * SIDE, SIDE, SIDE, 32, LANES), f32),
            jax.ShapeDtypeStruct((2, LANES), jnp.int32),
        ),
        in_specs=[smem] * 3 + [anywhere] * 6,
        out_specs=[anywhere, vmem],
        scratch_shapes=[
            pltpu.VMEM((3, 2 * SIDE, SIDE, SIDE, 32, LANES), f32),
            pltpu.VMEM(inverse.shape, f32),
            pltpu.VMEM((SIDE, archs * modes * 3 // 2, LANES), f32),
            pltpu.VMEM((SIDE, archs * LANES, LANES), f32),
            pltpu.VMEM(offset.shape, f32),
            pltpu.VMEM((instances, LANES, LANES), f32),
            pltpu.VMEM((count, 4 * modes, LANES), jnp.bfloat16),
            pltpu.VMEM((count, modes, LANES), f32),
            pltpu.VMEM((count, LANES, LANES), f32),
            pltpu.VMEM((count * 4, 32, LANES), f32),
            pltpu.VMEM((instances * 4, 32, LANES), f32),
            pltpu.VMEM((instances, LANES), f32),
            pltpu.VMEM(params.shape, f32),
            pltpu.SMEM(rows.shape, jnp.int32),
            pltpu.VMEM((16, LANES), jnp.int32),
            pltpu.SMEM((16, LANES), jnp.int32),
            pltpu.VMEM((3, SIDE, SIDE, 8, 32, LANES), f32),
            pltpu.VMEM((3, SIDE, SIDE, 8, 32, LANES), f32),
            pltpu.VMEM((3, SIDE, SIDE, 8, 32, LANES), f32),
            dma((7,)),
            dma((2, 3, 2)),
            dma((2, 3, 2)),
            dma((2, 3, 2, 3)),
            dma((2, 3, 2, 3)),
            dma((2, 3, 2)),
            dma((2, 3, 2)),
            dma((3, 2)),
            dma((3, 8)),
            dma((3, 3, 7)),
            dma((3, 3, 7)),
        ],
        compiler_params=pltpu.CompilerParams(
            collective_id=0, has_side_effects=True, vmem_limit_bytes=VMEM_LIMIT
        ),
        name="strips",
    )(arch, param, ports, rows, params, inverse, coupling, stiffness, offset)


AHEAD = 5


def assemble_kernel(where, arrived, out, even, odd, sems):
    step, steps = pl.program_id(0), pl.num_programs(0)

    def copies(at, slot):
        for r in range(8):
            for parity, buffer in enumerate((even, odd)):
                yield pltpu.make_async_copy(
                    arrived.at[where[(at * 8 + r) * 2 + parity]],
                    buffer.at[slot, pl.ds(r * 32, 32)],
                    sems.at[slot, parity, r],
                )

    @pl.when(step == 0)
    def _():
        for ahead in range(AHEAD):
            for copy in copies(ahead, ahead):
                copy.start()

    @pl.when(step + AHEAD < steps)
    def _():
        for copy in copies(step + AHEAD, (step + AHEAD) % (AHEAD + 1)):
            copy.start()

    slot = step % (AHEAD + 1)
    for copy in copies(step, slot):
        copy.wait()
    lane = lax.broadcasted_iota(jnp.int32, (8, LANES), 1)

    def row(i):
        e = even[slot, pl.ds(i, 8, stride=32), :]
        o = odd[slot, pl.ds(i, 8, stride=32), :]
        return jnp.where(lane < 32, e + o, e), o

    for g in range(8):
        (s0, o0), (s1, o1), (s2, o2), (s3, o3) = (row(4 * g + i) for i in range(4))
        if g == 0:
            s1 = jnp.where(lane == 0, pltpu.roll(s0, LANES - 1, 1), s1)
        tiles = (
            s0,
            pltpu.roll(jnp.where(lane < 32, s1, o0), 96, 1),
            jnp.where(lane < 96, pltpu.roll(s1, 96, 1), pltpu.roll(o1, 64, 1)),
            pltpu.roll(jnp.where(lane < 64, s2, o1), 64, 1),
            jnp.where(lane < 64, pltpu.roll(s2, 64, 1), pltpu.roll(o2, 32, 1)),
            pltpu.roll(jnp.where(lane < 96, s3, o2), 32, 1),
            jnp.where(lane < 32, pltpu.roll(s3, 32, 1), o3),
        )
        for t, tile in enumerate(tiles):
            out[:, (7 * g + t) * LANES : (7 * g + t + 1) * LANES] = tile


def assemble(where, arrived, ports):
    return pl.pallas_call(
        assemble_kernel,
        out_shape=jax.ShapeDtypeStruct((ports, 56 * LANES), jnp.float32),
        grid_spec=pltpu.PrefetchScalarGridSpec(
            num_scalar_prefetch=1,
            grid=(ports // 8,),
            in_specs=[pl.BlockSpec(memory_space=pl.ANY)],
            out_specs=pl.BlockSpec((8, 56 * LANES), lambda i, w: (i, 0)),
            scratch_shapes=[
                pltpu.VMEM((AHEAD + 1, 8 * 32, LANES), jnp.float32),
                pltpu.VMEM((AHEAD + 1, 8 * 32, LANES), jnp.float32),
                pltpu.SemaphoreType.DMA((AHEAD + 1, 2, 8)),
            ],
        ),
        compiler_params=pltpu.CompilerParams(vmem_limit_bytes=VMEM_LIMIT),
        name="assemble",
    )(where, arrived)


def body(
    instance_arch,
    instance_param,
    instance_ports,
    port_row,
    param_table,
    bubble_inverse,
    coupling,
    port_stiffness,
    coupling_offset,
):
    instances = instance_arch.shape[0]
    ports = 2 * instances
    archs, modes = coupling.shape[:2]
    arrived, where = strips_of(
        instance_arch,
        instance_param,
        instance_ports.T,
        port_row,
        param_table.T,
        bubble_inverse,
        coupling.reshape(archs * modes, LANES),
        port_stiffness.reshape(archs * LANES, LANES),
        coupling_offset,
    )
    return assemble(where.reshape(2 * ports), arrived.reshape(384, 32, LANES), ports)


def solution(mesh):
    return jax.shard_map(
        body,
        mesh=mesh,
        in_specs=(
            P(("inst", "arch")),
            P(("inst", "arch")),
            P(("inst", "arch"), None),
            P(),
            P(),
            P("arch", None, None),
            P("arch", None, None),
            P("arch", None, None),
            P(("inst", "arch"), None, None),
        ),
        out_specs=P(("inst", "arch"), None),
        check_vma=False,
    )
```

time: 177 us -> 124 us (0.70)
  Pallas kernels: 165 us -> 124 us
  local copies, waits for them, and re-layouts: 7.01 us -> 0 us
  other arithmetic: 3.82 us -> 0 us
    pallas_call x3 -> x1, Pallas kernels: 153 us -> 113 us  [strips_of(): pl.pallas_call(strips_kernel, out_shape=(jax.ShapeDtypeStruct((3, 2 * SID...]
    slice x2 -> x0, local copies, waits for them, and re-layouts: 3.46 us -> none  [the longest x1 2.44 us: body(): codes = arrived[:, 1, 0]]
    gather x2 -> x0, local copies, waits for them, and re-layouts: 2.32 us -> none  [the longest x1 1.72 us: body(): rows = jnp.take(port_row, instance_ports.reshape(count), axis=0)]
where the time goes in v2:
time: 124 us
  Pallas kernels  124 us (100%)
    pallas_call x1, Pallas kernels, strips_of(): pl.pallas_call(strips_kernel, out_shape=(jax.ShapeDtypeStruct((3, 2 * SID...  113 us
    pallas_call x1, Pallas kernels, assemble(): pl.pallas_call(assemble_kernel, out_shape=jax.ShapeDtypeStruct((ports, 56...  10.2 us

profile of v2, /device:TPU:1, one launch (start us, length us, event | category | flops | bytes accessed | tf_op | source)
XLA Modules:
  0.0 123.6 jit_solution(2214876095138287978)
XLA Ops:
  0.0 113.4 %strips.1 = (f32[3,8,4,4,32,128]{5,4,3,2,1,0:T(8,128)}, s32[2,128]{1,0:T(2,128)}) custom-call(s32[64]{0:T(128)} %arch.1, s32[64]{0:T(128)} %param.19, s32[4,64]{1,0:T(4,128)} %bitcast.10, s32[16384]{0:T(1024)} %row_in.1, f32[64,1024]{1,0:T(8,128)} %bitcast.9, f32[10,64,64]{2,1,0:T(8,128)} %inverse_in.1, f32[640,128]{1,0:T(8,128)} %bitcast.8, ...), custom_call_target="tpu_custom_call" | custom-call | tf_op jit(solution)/shard_map/strips/pallas_call | solution.py:452
  113.4 10.2 %assemble.1 = f32[128,7168]{1,0:T(8,128)} custom-call(s32[256]{0:T(256)} %bitcast.11, f32[384,32,128]{2,1,0:T(8,128)} %bitcast.6), custom_call_target="tpu_custom_call" | custom-call | tf_op jit(solution)/shard_map/assemble/pallas_call | solution.py:553

commit v3 on v2

--- a/solution.py
+++ b/solution.py
@@ -12,6 +12,7 @@
 OFFSETS = (1, 3, 2)
 LANES = 128
 VMEM_LIMIT = 56 << 20
+UNROLL = 16
 
 
 def position():
@@ -192,10 +193,7 @@
             both = jnp.concatenate(
                 [jnp.where(left_half, packed, flipped), jnp.where(left_half, flipped, packed)], axis=0
             )
-            high, low = halves(both)
-            inverse_table[plane * archs + at] = jnp.concatenate([high, high, low, low], axis=0).astype(
-                jnp.bfloat16
-            )
+            inverse_table[plane * archs + at] = both
             begin = pl.multiple_of(inverse_rows + at * modes, half_modes)
             c = basis[plane, pl.ds(begin, modes), :]
             natural[plane * archs + at] = c
@@ -211,7 +209,7 @@
                 stiff_table[(plane * archs + at) * 4 + k] = reorder(stiff[plane, pl.ds(begin, 32), :], k)
             return carry
 
-        lax.fori_loop(0, archs, one, 0)
+        lax.fori_loop(0, archs, one, 0, unroll=5)
 
     def turn(begin, end):
         def one(i, carry):
@@ -298,32 +296,38 @@
     along_z(1)
     own[3].wait()
     own[5].wait()
+    turn(0, instances)
+    basis_tables(z)
     look_up_scales()
-    basis_tables(z)
     to_other_core(0)
-    turn(0, instances // 2)
     along_lines(1)
-    turn(instances // 2, instances)
-    stiff_tables(z)
     for o in range(3):
         wait_plane(0, o)
         basis_tables(planes[o])
     to_other_core(1)
 
+    left_modes = left[:modes]
+
     def condense(step, carry):
-        for u in range(4):
-            i = step * 4 + u
+        applied = []
+        for u in range(UNROLL):
+            i = step * UNROLL + u
             a = arch[i]
-            scale = scales[pl.ds(i, 1), :]
-            weighted = (coupling_table[a] + turned[i]) * scale
+            scaled = inverse_table[a] * scales[pl.ds(i, 1), :]
+            mixed = jnp.where(left_modes, scaled, halves(scaled)[1]).astype(jnp.bfloat16)
+            high, low = halves(natural[a] + offset[i])
+            applied.append(
+                jnp.dot(
+                    jnp.concatenate([mixed, mixed], axis=1),
+                    jnp.concatenate([high, high, low, low], axis=0).astype(jnp.bfloat16),
+                    preferred_element_type=jnp.float32,
+                )
+            )
+        for u in range(UNROLL):
+            i = step * UNROLL + u
+            high, low = halves(applied[u])
+            weighted = (coupling_table[arch[i]] + turned[i]) * scales[pl.ds(i, 1), :]
             mixed = jnp.where(left, weighted, halves(weighted)[1]).astype(jnp.bfloat16)
-            applied = scale * jnp.dot(
-                jnp.concatenate([mixed, mixed], axis=1),
-                inverse_table[a],
-                preferred_element_type=jnp.float32,
-            )
-            mixed = jnp.where(left, applied, halves(applied)[1]).astype(jnp.bfloat16)
-            high, low = halves(natural[a] + offset[i])
             product = jnp.dot(
                 jnp.concatenate([mixed, mixed], axis=1),
                 jnp.concatenate([high, high, low, low], axis=0).astype(jnp.bfloat16),
@@ -333,7 +337,8 @@
                 strips[k * instances + i] = reorder(product[k * 32 : (k + 1) * 32], k)
         return carry
 
-    lax.fori_loop(0, instances // 4, condense, 0)
+    lax.fori_loop(0, instances // UNROLL, condense, 0)
+    stiff_tables(z)
     for o in range(3):
         wait_plane(1, o)
         stiff_tables(planes[o])
@@ -464,7 +469,7 @@
             pltpu.VMEM((SIDE, archs * LANES, LANES), f32),
             pltpu.VMEM(offset.shape, f32),
             pltpu.VMEM((instances, LANES, LANES), f32),
-            pltpu.VMEM((count, 4 * modes, LANES), jnp.bfloat16),
+            pltpu.VMEM((count, modes, LANES), f32),
             pltpu.VMEM((count, modes, LANES), f32),
             pltpu.VMEM((count, LANES, LANES), f32),
             pltpu.VMEM((count * 4, 32, LANES), f32),
@@ -496,74 +501,82 @@
     )(arch, param, ports, rows, params, inverse, coupling, stiffness, offset)
 
 
-AHEAD = 5
-
-
-def assemble_kernel(where, arrived, out, even, odd, sems):
-    step, steps = pl.program_id(0), pl.num_programs(0)
-
-    def copies(at, slot):
+AHEAD = 12
+
+
+def assemble_kernel(where, arrived, out, even, odd, rows, in_sems, out_sems):
+    groups = rows.shape[0]
+
+    def fetch(group):
         for r in range(8):
             for parity, buffer in enumerate((even, odd)):
-                yield pltpu.make_async_copy(
-                    arrived.at[where[(at * 8 + r) * 2 + parity]],
-                    buffer.at[slot, pl.ds(r * 32, 32)],
-                    sems.at[slot, parity, r],
-                )
-
-    @pl.when(step == 0)
-    def _():
-        for ahead in range(AHEAD):
-            for copy in copies(ahead, ahead):
-                copy.start()
-
-    @pl.when(step + AHEAD < steps)
-    def _():
-        for copy in copies(step + AHEAD, (step + AHEAD) % (AHEAD + 1)):
-            copy.start()
-
-    slot = step % (AHEAD + 1)
-    for copy in copies(step, slot):
-        copy.wait()
+                pltpu.make_async_copy(
+                    arrived.at[where[(group * 8 + r) * 2 + parity]],
+                    buffer.at[group, :, r],
+                    in_sems.at[group, parity],
+                ).start()
+
+    def written(group):
+        begin = pl.multiple_of(group * 8, 8)
+        return pltpu.make_async_copy(rows.at[group], out.at[pl.ds(begin, 8)], out_sems.at[group])
+
     lane = lax.broadcasted_iota(jnp.int32, (8, LANES), 1)
-
-    def row(i):
-        e = even[slot, pl.ds(i, 8, stride=32), :]
-        o = odd[slot, pl.ds(i, 8, stride=32), :]
-        return jnp.where(lane < 32, e + o, e), o
-
-    for g in range(8):
-        (s0, o0), (s1, o1), (s2, o2), (s3, o3) = (row(4 * g + i) for i in range(4))
-        if g == 0:
-            s1 = jnp.where(lane == 0, pltpu.roll(s0, LANES - 1, 1), s1)
-        tiles = (
-            s0,
-            pltpu.roll(jnp.where(lane < 32, s1, o0), 96, 1),
-            jnp.where(lane < 96, pltpu.roll(s1, 96, 1), pltpu.roll(o1, 64, 1)),
-            pltpu.roll(jnp.where(lane < 64, s2, o1), 64, 1),
-            jnp.where(lane < 64, pltpu.roll(s2, 64, 1), pltpu.roll(o2, 32, 1)),
-            pltpu.roll(jnp.where(lane < 96, s3, o2), 32, 1),
-            jnp.where(lane < 32, pltpu.roll(s3, 32, 1), o3),
-        )
-        for t, tile in enumerate(tiles):
-            out[:, (7 * g + t) * LANES : (7 * g + t + 1) * LANES] = tile
+    for group in range(AHEAD):
+        fetch(group)
+
+    def lay_out(group, carry):
+        @pl.when(group + AHEAD < groups)
+        def _():
+            fetch(group + AHEAD)
+
+        take(even.at[group], in_sems.at[group, 0])
+        take(odd.at[group], in_sems.at[group, 1])
+
+        def row(i):
+            e, o = even[group, i], odd[group, i]
+            return jnp.where(lane < 32, e + o, e), o
+
+        for g in range(8):
+            (s0, o0), (s1, o1), (s2, o2), (s3, o3) = (row(4 * g + i) for i in range(4))
+            if g == 0:
+                s1 = jnp.where(lane == 0, pltpu.roll(s0, LANES - 1, 1), s1)
+            tiles = (
+                s0,
+                pltpu.roll(jnp.where(lane < 32, s1, o0), 96, 1),
+                jnp.where(lane < 96, pltpu.roll(s1, 96, 1), pltpu.roll(o1, 64, 1)),
+                pltpu.roll(jnp.where(lane < 64, s2, o1), 64, 1),
+                jnp.where(lane < 64, pltpu.roll(s2, 64, 1), pltpu.roll(o2, 32, 1)),
+                pltpu.roll(jnp.where(lane < 96, s3, o2), 32, 1),
+                jnp.where(lane < 32, pltpu.roll(s3, 32, 1), o3),
+            )
+            for t, tile in enumerate(tiles):
+                rows[group, :, (7 * g + t) * LANES : (7 * g + t + 1) * LANES] = tile
+        written(group).start()
+        return carry
+
+    lax.fori_loop(0, groups, lay_out, 0)
+
+    def finish(group, carry):
+        written(group).wait()
+        return carry
+
+    lax.fori_loop(0, groups, finish, 0)
 
 
 def assemble(where, arrived, ports):
+    groups = ports // 8
     return pl.pallas_call(
         assemble_kernel,
         out_shape=jax.ShapeDtypeStruct((ports, 56 * LANES), jnp.float32),
-        grid_spec=pltpu.PrefetchScalarGridSpec(
-            num_scalar_prefetch=1,
-            grid=(ports // 8,),
-            in_specs=[pl.BlockSpec(memory_space=pl.ANY)],
-            out_specs=pl.BlockSpec((8, 56 * LANES), lambda i, w: (i, 0)),
-            scratch_shapes=[
-                pltpu.VMEM((AHEAD + 1, 8 * 32, LANES), jnp.float32),
-                pltpu.VMEM((AHEAD + 1, 8 * 32, LANES), jnp.float32),
-                pltpu.SemaphoreType.DMA((AHEAD + 1, 2, 8)),
-            ],
-        ),
+        in_specs=[pl.BlockSpec(memory_space=pltpu.SMEM), pl.BlockSpec(memory_space=pl.ANY)],
+        out_specs=pl.BlockSpec(memory_space=pl.ANY),
+        scratch_shapes=[
+            pltpu.VMEM((groups, 32, 8, LANES), jnp.float32),
+            pltpu.VMEM((groups, 32, 8, LANES), jnp.float32),
+            pltpu.VMEM((groups, 8, 56 * LANES), jnp.float32),
+            pltpu.SemaphoreType.DMA((groups, 2)),
+            pltpu.SemaphoreType.DMA((groups,)),
+        ],
         compiler_params=pltpu.CompilerParams(vmem_limit_bytes=VMEM_LIMIT),
         name="assemble",
     )(where, arrived)

time: 124 us -> 112 us (0.903)
  Pallas kernels: 124 us -> 112 us
    pallas_call x1, Pallas kernels: 113 us -> 107 us  [strips_of(): pl.pallas_call(strips_kernel, out_shape=(jax.ShapeDtypeStruct((3, 2 * SID...]
    pallas_call x1, Pallas kernels: 10.2 us -> 5.11 us  [assemble(): pl.pallas_call(assemble_kernel, out_shape=jax.ShapeDtypeStruct((ports, 56...]
where the time goes in v3:
time: 112 us
  Pallas kernels  112 us (100%)
    pallas_call x1, Pallas kernels, strips_of(): pl.pallas_call(strips_kernel, out_shape=(jax.ShapeDtypeStruct((3, 2 * SID...  107 us
    pallas_call x1, Pallas kernels, assemble(): pl.pallas_call(assemble_kernel, out_shape=jax.ShapeDtypeStruct((ports, 56...  5.11 us

profile of v3, /device:TPU:1, one launch (start us, length us, event | category | flops | bytes accessed | tf_op | source)
XLA Modules:
  0.0 111.8 jit_solution(17353572109864435261)
XLA Ops:
  0.0 106.6 %strips.1 = (f32[3,8,4,4,32,128]{5,4,3,2,1,0:T(8,128)}, s32[2,128]{1,0:T(2,128)}) custom-call(s32[64]{0:T(128)} %arch.1, s32[64]{0:T(128)} %param.19, s32[4,64]{1,0:T(4,128)} %bitcast.10, s32[16384]{0:T(1024)} %row_in.1, f32[64,1024]{1,0:T(8,128)} %bitcast.9, f32[10,64,64]{2,1,0:T(8,128)} %inverse_in.1, f32[640,128]{1,0:T(8,128)} %bitcast.8, ...), custom_call_target="tpu_custom_call" | custom-call | tf_op jit(solution)/shard_map/strips/pallas_call | solution.py:457
  106.6 5.1 %assemble.1 = f32[128,7168]{1,0:T(8,128)} custom-call(s32[256]{0:T(256)} %bitcast.11, f32[384,32,128]{2,1,0:T(8,128)} %bitcast.6), custom_call_target="tpu_custom_call" | custom-call | tf_op jit(solution)/shard_map/assemble/pallas_call | solution.py:568

commit v4 on v3

--- a/solution.py
+++ b/solution.py
@@ -107,7 +107,9 @@
     r3,
     here_sems,
     out_sems,
-    ss,
+    ss1,
+    ss2,
+    ss3,
     rs,
 ):
     here = position()
@@ -200,7 +202,7 @@
             coupling_table[plane * archs + at] = jnp.concatenate([c, c], axis=0).T
             return carry
 
-        lax.fori_loop(0, archs, one, 0, unroll=2)
+        lax.fori_loop(0, archs, one, 0, unroll=5)
 
     def stiff_tables(plane):
         def one(at, carry):
@@ -217,7 +219,7 @@
             turned[i] = jnp.concatenate([v, v], axis=0).T
             return carry
 
-        lax.fori_loop(begin, end, one, 0, unroll=2)
+        lax.fori_loop(begin, end, one, 0, unroll=8)
 
     def look_up_scales():
         wanted = jnp.zeros((8, LANES), jnp.int32)
@@ -356,80 +358,78 @@
             into[i // 8, i % 8, :8] = jnp.where(spot, slots[part + 3, at].astype(jnp.float32), top)
             return carry
 
-        lax.fori_loop(0, 32, one, 0, unroll=4)
-
-    copies = []
+        lax.fori_loop(0, 32, one, 0, unroll=8)
+
     for i, o in enumerate(OFFSETS):
         for part, (a1, a2, a3) in enumerate(ORDERS):
             line = (here[a1] + o) % SIDE
             pack(part, line, first.at[part, line])
+            there = moved(here, a1, o)
             sent.append(
                 send(
                     first.at[part, line],
                     second.at[part, here[a1]],
-                    ss.at[part, 0, i],
+                    ss1.at[part, i],
                     rs.at[part, 0, i],
-                    moved(here, a1, o),
+                    there,
                 )
             )
     for part, (a1, a2, a3) in enumerate(ORDERS):
         pack(part, here[a1], second.at[part, here[a1]])
-    for part, (a1, a2, a3) in enumerate(ORDERS):
-        for i, o in enumerate(OFFSETS):
-            take(second.at[part, 0], rs.at[part, 0, i])
-        for i, o in enumerate(OFFSETS):
-            line = (here[a2] + o) % SIDE
-            sent.append(
-                send(
-                    second.at[part, :, line],
-                    third.at[part, here[a2]],
-                    ss.at[part, 1, i],
-                    rs.at[part, 1, i],
-                    moved(here, a2, o),
-                )
-            )
-        copy = pltpu.make_async_copy(
-            second.at[part, :, here[a2]], third.at[part, here[a2]], here_sems.at[part, 0]
-        )
-        copy.start()
-        copies.append(copy)
-    for part, (a1, a2, a3) in enumerate(ORDERS):
-        copies[part].wait()
-        for i, o in enumerate(OFFSETS):
-            take(third.at[part, 0], rs.at[part, 1, i])
-        mine = here[a3] * 2 + core
-        n = 0
-        for o in (*OFFSETS, 0):
-            for flip in (0, 1):
-                there = moved(here, a3, o)
-                to = (core + flip) % 2
-                there = (there[0], there[1], to, there[3])
-                src = third.at[part, :, :, there[a3] * 2 + to]
-                dst = arrived.at[part, mine]
-                if o == 0 and flip == 0:
-                    copy = pltpu.make_async_copy(src, dst, here_sems.at[part, 1])
-                    copy.start()
-                    copies.append(copy)
-                else:
-                    sent.append(send(src, dst, ss.at[part, 2, n], rs.at[part, 2, n], there))
-                    n += 1
+    kept = [[], [], []]
+    for n, o in enumerate((0, *OFFSETS)):
+        for part, (a1, a2, a3) in enumerate(ORDERS):
+            source = (here[a1] + SIDE - o) % SIDE
+            if o:
+                take(second.at[part, source], rs.at[part, 0, n - 1])
+            dst = third.at[part, here[a2], source]
+            for i, p in enumerate(OFFSETS):
+                there = moved(here, a2, p)
+                src = second.at[part, source, there[a2]]
+                sent.append(send(src, dst, ss2.at[part, i, n], rs.at[part, 1, i], there))
+            copy = pltpu.make_async_copy(
+                second.at[part, source, here[a2]], dst, here_sems.at[part, 0, n]
+            )
+            copy.start()
+            kept[part].append(copy)
+    own_strips = [[], [], []]
+    for n, o in enumerate((0, *OFFSETS)):
+        for part, (a1, a2, a3) in enumerate(ORDERS):
+            source = (here[a2] + SIDE - o) % SIDE
+            if o:
+                take(third.at[part, source], rs.at[part, 1, n - 1])
+            else:
+                for copy in kept[part]:
+                    copy.wait()
+            dst = arrived.at[part, here[a3] * 2 + core, source]
+            i = 0
+            for p in (*OFFSETS, 0):
+                for flip in (0, 1):
+                    there = moved(here, a3, p)
+                    to = (core + flip) % 2
+                    there = (there[0], there[1], to, there[3])
+                    src = third.at[part, source, :, there[a3] * 2 + to]
+                    if p == 0 and flip == 0:
+                        copy = pltpu.make_async_copy(src, dst, here_sems.at[part, 1, n])
+                        copy.start()
+                        own_strips[part].append(copy)
+                    else:
+                        sent.append(send(src, dst, ss3.at[part, i, n], rs.at[part, 2, i], there))
+                        i += 1
     out = []
-    for part, (a1, a2, a3) in enumerate(ORDERS):
-        mine = here[a3] * 2 + core
-        n = 0
-        for o in (0, *OFFSETS):
-            for flip in (0, 1):
-                origin = (here[a3] + SIDE - o) % SIDE * 2 + (core + flip) % 2
-                if o == 0 and flip == 0:
-                    copies[3 + part].wait()
-                else:
-                    take(arrived.at[part, origin], rs.at[part, 2, (n + 6) % 7])
-                    n += 1
-                copy = pltpu.make_async_copy(
-                    arrived.at[part, origin], arrived_out.at[part, origin], out_sems.at[part, n]
-                )
-                copy.start()
-                out.append(copy)
+    for n, (o, flip) in enumerate([(o, flip) for o in (0, *OFFSETS) for flip in (0, 1)]):
+        for part, (a1, a2, a3) in enumerate(ORDERS):
+            origin = (here[a3] + SIDE - o) % SIDE * 2 + (core + flip) % 2
+            if n == 0:
+                for copy in own_strips[part]:
+                    copy.wait()
+            else:
+                take(arrived.at[part, origin], rs.at[part, 2, (n + 5) % 7])
+            copy = pltpu.make_async_copy(
+                arrived.at[part, origin], arrived_out.at[part, origin], out_sems.at[part, n]
+            )
+            copy.start()
+            out.append(copy)
     landed = arrived.reshape(384 * 32, LANES)
     found = [jnp.zeros((8, LANES), jnp.int32)] * 2
     for g in range(48):
@@ -489,9 +489,11 @@
             dma((2, 3, 2, 3)),
             dma((2, 3, 2)),
             dma((2, 3, 2)),
-            dma((3, 2)),
+            dma((3, 2, 4)),
             dma((3, 8)),
-            dma((3, 3, 7)),
+            dma((3, 3)),
+            dma((3, 3, 4)),
+            dma((3, 7, 4)),
             dma((3, 3, 7)),
         ],
         compiler_params=pltpu.CompilerParams(
@@ -501,7 +503,7 @@
     )(arch, param, ports, rows, params, inverse, coupling, stiffness, offset)
 
 
-AHEAD = 12
+AHEAD = 16
 
 
 def assemble_kernel(where, arrived, out, even, odd, rows, in_sems, out_sems):

time: 112 us -> 110 us (0.982)
  Pallas kernels: 112 us -> 110 us
    pallas_call x1, Pallas kernels: 107 us -> 105 us  [strips_of(): pl.pallas_call(strips_kernel, out_shape=(jax.ShapeDtypeStruct((3, 2 * SID...]
where the time goes in v4:
time: 110 us
  Pallas kernels  110 us (100%)
    pallas_call x1, Pallas kernels, strips_of(): pl.pallas_call(strips_kernel, out_shape=(jax.ShapeDtypeStruct((3, 2 * SID...  105 us
    pallas_call x1, Pallas kernels, assemble(): pl.pallas_call(assemble_kernel, out_shape=jax.ShapeDtypeStruct((ports, 56...  5.03 us

profile of v4, /device:TPU:1, one launch (start us, length us, event | category | flops | bytes accessed | tf_op | source)
XLA Modules:
  0.0 109.9 jit_solution(17332216939430943858)
XLA Ops:
  0.0 104.9 %strips.1 = (f32[3,8,4,4,32,128]{5,4,3,2,1,0:T(8,128)}, s32[2,128]{1,0:T(2,128)}) custom-call(s32[64]{0:T(128)} %arch.1, s32[64]{0:T(128)} %param.19, s32[4,64]{1,0:T(4,128)} %bitcast.10, s32[16384]{0:T(1024)} %row_in.1, f32[64,1024]{1,0:T(8,128)} %bitcast.9, f32[10,64,64]{2,1,0:T(8,128)} %inverse_in.1, f32[640,128]{1,0:T(8,128)} %bitcast.8, ...), custom_call_target="tpu_custom_call" | custom-call | tf_op jit(solution)/shard_map/strips/pallas_call | solution.py:457
  104.9 5.0 %assemble.1 = f32[128,7168]{1,0:T(8,128)} custom-call(s32[256]{0:T(256)} %bitcast.11, f32[384,32,128]{2,1,0:T(8,128)} %bitcast.6), custom_call_target="tpu_custom_call" | custom-call | tf_op jit(solution)/shard_map/assemble/pallas_call | solution.py:570

commit v5 on v4

--- a/solution.py
+++ b/solution.py
@@ -188,6 +188,11 @@
         for half in (0, 1):
             take(core_half(a, half, planes[o], 1 - core), r3.at[a, o, half])
 
+    def doubled(one, other):
+        both = jnp.concatenate([one, other], axis=0).T
+        flipped = pltpu.roll(both, modes, 1)
+        return jnp.where(left, both, flipped), jnp.where(left, flipped, both)
+
     def basis_tables(plane):
         def one(at, carry):
             packed = basis[plane, pl.ds(pl.multiple_of(at * half_modes, half_modes), half_modes), :]
@@ -196,13 +201,20 @@
                 [jnp.where(left_half, packed, flipped), jnp.where(left_half, flipped, packed)], axis=0
             )
             inverse_table[plane * archs + at] = both
-            begin = pl.multiple_of(inverse_rows + at * modes, half_modes)
+            return carry
+
+        lax.fori_loop(0, archs, one, 0, unroll=5)
+
+        def two(pair, carry):
+            begin = pl.multiple_of(inverse_rows + pair * 2 * modes, half_modes)
             c = basis[plane, pl.ds(begin, modes), :]
-            natural[plane * archs + at] = c
-            coupling_table[plane * archs + at] = jnp.concatenate([c, c], axis=0).T
+            d = basis[plane, pl.ds(pl.multiple_of(begin + modes, half_modes), modes), :]
+            at = plane * archs + pair * 2
+            natural[at], natural[at + 1] = c, d
+            coupling_table[at], coupling_table[at + 1] = doubled(c, d)
             return carry
 
-        lax.fori_loop(0, archs, one, 0, unroll=5)
+        lax.fori_loop(0, archs // 2, two, 0, unroll=5)
 
     def stiff_tables(plane):
         def one(at, carry):
@@ -215,11 +227,12 @@
 
     def turn(begin, end):
         def one(i, carry):
-            v = offset[i]
-            turned[i] = jnp.concatenate([v, v], axis=0).T
+            first_of_two, second_of_two = doubled(offset[2 * i], offset[2 * i + 1])
+            turned[2 * i] = first_of_two
+            turned[2 * i + 1] = second_of_two
             return carry
 
-        lax.fori_loop(begin, end, one, 0, unroll=8)
+        lax.fori_loop(begin // 2, end // 2, one, 0, unroll=4)
 
     def look_up_scales():
         wanted = jnp.zeros((8, LANES), jnp.int32)
@@ -290,12 +303,12 @@
 
     along_z(0)
     own[2].wait()
+    along_z(1)
     own[4].wait()
     place_strips()
     to_scalars = pltpu.make_async_copy(slots_vector, slots, local.at[6])
     to_scalars.start()
     along_lines(0)
-    along_z(1)
     own[3].wait()
     own[5].wait()
     turn(0, instances)
@@ -416,6 +429,8 @@
                     else:
                         sent.append(send(src, dst, ss3.at[part, i, n], rs.at[part, 2, i], there))
                         i += 1
+    landed = arrived.reshape(384 * 32, LANES)
+    found = [jnp.zeros((8, LANES), jnp.int32)] * 2
     out = []
     for n, (o, flip) in enumerate([(o, flip) for o in (0, *OFFSETS) for flip in (0, 1)]):
         for part, (a1, a2, a3) in enumerate(ORDERS):
@@ -430,13 +445,12 @@
             )
             copy.start()
             out.append(copy)
-    landed = arrived.reshape(384 * 32, LANES)
-    found = [jnp.zeros((8, LANES), jnp.int32)] * 2
-    for g in range(48):
-        codes = landed[pl.ds(g * 256 + 1, 8, stride=32), :][:, :1]
-        for t in (0, 1):
-            hit = codes == (lane8 + t * LANES).astype(jnp.float32)
-            found[t] = found[t] + jnp.where(hit, row8 + g * 8, 0)
+            strip = (part * 2 * SIDE + origin) * SIDE * SIDE
+            for g in (0, 8):
+                codes = landed[pl.ds((strip + g) * 32 + 1, 8, stride=32), :][:, :1]
+                for t in (0, 1):
+                    hit = codes == (lane8 + t * LANES).astype(jnp.float32)
+                    found[t] = found[t] + jnp.where(hit, row8 + (strip + g), 0)
     for t in (0, 1):
         where[t : t + 1, :] = jnp.sum(found[t], axis=0, keepdims=True)
     for copy in sent:
@@ -450,7 +464,7 @@
     archs, modes = inverse.shape[:2]
     instances, count = offset.shape[0], SIDE * archs
     f32 = jnp.float32
-    assert archs * modes * 3 // 2 == 8 * sum(PIECES[0]) and archs * LANES == 8 * sum(PIECES[1])
+    assert archs % 2 == 0 and archs * modes * 3 // 2 == 8 * sum(PIECES[0]) and archs * LANES == 8 * sum(PIECES[1])
     smem, vmem, anywhere = (
         pl.BlockSpec(memory_space=m) for m in (pltpu.SMEM, pltpu.VMEM, pl.ANY)
     )

time: 110 us -> 110 us (level)
  no operation moved by 1% of the time
where the time goes in v5:
time: 110 us
  Pallas kernels  110 us (100%)
    pallas_call x1, Pallas kernels, strips_of(): pl.pallas_call(strips_kernel, out_shape=(jax.ShapeDtypeStruct((3, 2 * SID...  105 us
    pallas_call x1, Pallas kernels, assemble(): pl.pallas_call(assemble_kernel, out_shape=jax.ShapeDtypeStruct((ports, 56...  5.03 us

profile of v5, /device:TPU:1, one launch (start us, length us, event | category | flops | bytes accessed | tf_op | source)
XLA Modules:
  0.0 109.6 jit_solution(4125559889400498529)
XLA Ops:
  0.0 104.6 %strips.1 = (f32[3,8,4,4,32,128]{5,4,3,2,1,0:T(8,128)}, s32[2,128]{1,0:T(2,128)}) custom-call(s32[64]{0:T(128)} %arch.1, s32[64]{0:T(128)} %param.19, s32[4,64]{1,0:T(4,128)} %bitcast.10, s32[16384]{0:T(1024)} %row_in.1, f32[64,1024]{1,0:T(8,128)} %bitcast.9, f32[10,64,64]{2,1,0:T(8,128)} %inverse_in.1, f32[640,128]{1,0:T(8,128)} %bitcast.8, ...), custom_call_target="tpu_custom_call" | custom-call | tf_op jit(solution)/shard_map/strips/pallas_call | solution.py:471
  104.6 5.0 %assemble.1 = f32[128,7168]{1,0:T(8,128)} custom-call(s32[256]{0:T(256)} %bitcast.11, f32[384,32,128]{2,1,0:T(8,128)} %bitcast.6), custom_call_target="tpu_custom_call" | custom-call | tf_op jit(solution)/shard_map/assemble/pallas_call | solution.py:584
